TPU v7x, 128 devices: a whole 4x4x4 slice. The times are simulated.
128 devices in a mesh: gx: 16 (over y, z), gy: 8 (over x, core).
Axes of the slice: x: 4, y: 4, z: 4, core: 2. Of those that a mesh axis runs over, the one named last changes fastest.
Arguments:
- pressure: float32 [12, 512, 1024], P(None, 'gx', 'gy'), may hold values from 0.5 to 1.5
- saturation: float32 [2, 12, 512, 1024], P(None, None, 'gx', 'gy'), may hold values from 0.05 to 0.35
- permeability: float32 [3, 12, 512, 1024], P(None, None, 'gx', 'gy'), may hold values from 0.25 to 8
- pore_volume: float32 [12, 512, 1024], P(None, 'gx', 'gy'), may hold values from 0.5 to 8
- cell_depth: float32 [12, 512, 1024], P(None, 'gx', 'gy'), may hold values from -4 to 4
- residual: float32 [3, 12, 512, 1024], P(None, None, 'gx', 'gy'), may hold values from -12 to 12
- upstream_flags: int32 [12, 512, 1024], P(None, 'gx', 'gy'), may hold values from 0 to 7
- perf_cell: int32 [128, 1024], P(('gx', 'gy')), may hold values from 0 to 49151
- perf_well: int32 [128, 1024], P(('gx', 'gy')), may hold values from -1 to 4095, as said below
- perf_index: float32 [128, 1024], P(('gx', 'gy')), may hold values from 0.5 to 4
- well_mode: int32 [4096], P(('gx', 'gy')), may hold values from 0 to 1
- well_target: float32 [4096], P(('gx', 'gy')), may hold values from 0.2 to 1.2
Outputs:
- new_pressure: float32 [12, 512, 1024], P(None, 'gx', 'gy')
- well_bhp: float32 [4096], P(('gx', 'gy'))
Inputs may be any that keep to these rules, and one draw needn't show every extreme that they name: `upstream_flags`: bit 1 set: the cell is upstream on its face towards the next cell along x; bit 2: along y; bit 4: along z. `perf_cell`: the local cell number, within its row's block of columns, of the perforated cell. `perf_well`: -1 marks an empty slot; in each row the live slots come first; every well has at least one live slot; in every draw some row has all 1024 slots live. `well_mode`: 0: the well holds its bottom-hole pressure at well_target; 1: it produces well_target.
All inputs are finite; a program needn't handle non-finite values.
Results may differ from a plain program's by a relative error of at most 0.0003.
Values sent between devices are 32-bit elements; how exact they have to be, the bound alone decides.
A program may use at most 64 MiB of HBM per device.

v0:
```python
import jax
import jax.numpy as jnp
from jax import lax
from jax.sharding import PartitionSpec as P

SWEEPS = 2


MU_OIL = 2.0
MU_WATER = 1.0
MU_GAS = 0.2
COMP_OIL = 0.2
COMP_WATER = 0.05
GRAV_OIL = 0.4
GRAV_WATER = 0.5
GRAV_GAS = 0.08
RELAXATION = 0.8


def extended(cells, sides, width):
    for axis, dim in sides:
        count = lax.axis_size(axis)
        ends = count - 1
        head = lax.slice_in_dim(cells, 0, width, axis=dim)
        tail = lax.slice_in_dim(cells, cells.shape[dim] - width, cells.shape[dim], axis=dim)
        cells = jnp.concatenate(
            [
                lax.ppermute(tail, axis, [(i, (i + 1) % count) for i in range(ends)]),
                cells,
                lax.ppermute(head, axis, [((i + 1) % count, i) for i in range(ends)]),
            ],
            axis=dim,
        )
    return cells


def phase_weights(pressure):
    b_oil = 1.0 + COMP_OIL * (pressure - 1.0)
    b_water = 1.0 + COMP_WATER * (pressure - 1.0)
    return (1.0 / b_oil, 1.0 / b_water, 1.0 / pressure)


def phase_mobility(pressure, sat_water, sat_gas):
    sat_oil = 1.0 - sat_water - sat_gas
    b_oil = 1.0 + COMP_OIL * (pressure - 1.0)
    b_water = 1.0 + COMP_WATER * (pressure - 1.0)
    return (
        sat_oil * sat_oil * b_oil / MU_OIL,
        sat_water * sat_water * b_water / MU_WATER,
        sat_gas * sat_gas * pressure / MU_GAS,
    )


def storage_term(weights, sat_water, sat_gas):
    sat_oil = 1.0 - sat_water - sat_gas
    return (
        sat_oil * COMP_OIL * weights[0] + sat_water * COMP_WATER * weights[1] + sat_gas * weights[2]
    )


def flag_bits(flag_code):
    bit_x = jnp.mod(flag_code, 2.0)
    remainder = (flag_code - bit_x) * 0.5
    bit_y = jnp.mod(remainder, 2.0)
    return (bit_x, bit_y, (remainder - bit_y) * 0.5)


def face_terms(weights, mob_center, mob_beside, perm_center, perm_beside, center_up, depth_drop):
    transmit = 2.0 * perm_center * perm_beside / (perm_center + perm_beside)
    coupling = jnp.zeros_like(transmit)
    gravity = jnp.zeros_like(transmit)
    for weight, center, beside, lift_rate in zip(
        weights, mob_center, mob_beside, (GRAV_OIL, GRAV_WATER, GRAV_GAS)
    ):
        flux_term = weight * (transmit * jnp.where(center_up, center, beside))
        coupling = coupling + flux_term
        gravity = gravity + flux_term * lift_rate
    return (coupling, gravity * depth_drop)


def direction_terms(weights, center, plus_side, minus_side, bit_center, bit_minus):
    coup_plus, grav_plus = face_terms(
        weights,
        center[0],
        plus_side[0],
        center[1],
        plus_side[1],
        bit_center > 0.5,
        center[2] - plus_side[2],
    )
    coup_minus, grav_minus = face_terms(
        weights,
        center[0],
        minus_side[0],
        center[1],
        minus_side[1],
        bit_minus < 0.5,
        center[2] - minus_side[2],
    )
    return ((coup_plus, coup_minus), grav_plus + grav_minus)


def neighbour(grid_field, axis_dim, offset):
    padding = [(0, 0)] * grid_field.ndim
    padding[axis_dim] = (1, 1)
    padded = jnp.pad(grid_field, padding)
    return lax.slice_in_dim(
        padded, 1 + offset, 1 + offset + grid_field.shape[axis_dim], axis=axis_dim
    )


def plus_minus(rim_field, direction):
    if direction == 0:
        return (rim_field[:, 2:, 1:-1], rim_field[:, :-2, 1:-1])
    return (rim_field[:, 1:-1, 2:], rim_field[:, 1:-1, :-2])


def coupled_sum(couplings, besides):
    running = couplings[0] * besides[0]
    for coupling, beside in zip(couplings[1:], besides[1:]):
        running = running + coupling * beside
    return running


def body(
    pressure,
    saturation,
    permeability,
    pore_volume,
    cell_depth,
    residual,
    upstream_flags,
    perf_cell,
    perf_well,
    perf_index,
    well_mode,
    well_target,
):
    sat_water, sat_gas = (saturation[0], saturation[1])
    weights = phase_weights(pressure)
    mobility = phase_mobility(pressure, sat_water, sat_gas)
    storage = pore_volume * storage_term(weights, sat_water, sat_gas)
    flag_code = upstream_flags.astype(jnp.float32)
    flag_parts = flag_bits(flag_code)
    planes = jnp.stack(
        mobility + (pressure, permeability[0], permeability[1], cell_depth, flag_code)
    )
    rimmed = extended(planes, (("gx", 2), ("gy", 3)), 1)
    rim_sets = [
        (rimmed[0], rimmed[1], rimmed[2], rimmed[3], rimmed[4 + direction], rimmed[6], rimmed[7])
        for direction in range(2)
    ]
    couplings = ()
    gravity = jnp.zeros_like(pressure)
    for direction in range(3):
        if direction < 2:
            fields = rim_sets[direction]
            mob_sides = [plus_minus(fields[index], direction) for index in range(3)]
            perm_sides = plus_minus(fields[4], direction)
            depth_sides = plus_minus(fields[5], direction)
            bit_minus = flag_bits(plus_minus(fields[6], direction)[1])[direction]
        else:
            mob_sides = [
                (neighbour(phase_field, 0, 1), neighbour(phase_field, 0, -1))
                for phase_field in mobility
            ]
            perm_sides = (neighbour(permeability[2], 0, 1), neighbour(permeability[2], 0, -1))
            depth_sides = (neighbour(cell_depth, 0, 1), neighbour(cell_depth, 0, -1))
            bit_minus = neighbour(flag_parts[2], 0, -1)
        center = (mobility, permeability[direction], cell_depth)
        plus_side = (tuple((sides[0] for sides in mob_sides)), perm_sides[0], depth_sides[0])
        minus_side = (tuple((sides[1] for sides in mob_sides)), perm_sides[1], depth_sides[1])
        coupled, grav_part = direction_terms(
            weights, center, plus_side, minus_side, flag_parts[direction], bit_minus
        )
        couplings = couplings + coupled
        gravity = gravity + grav_part
    first_besides = plus_minus(rim_sets[0][3], 0) + plus_minus(rim_sets[1][3], 1)
    faces_total = (
        couplings[0] + couplings[1] + couplings[2] + couplings[3] + couplings[4] + couplings[5]
    )
    combined = weights[0] * residual[0] + weights[1] * residual[1] + weights[2] * residual[2]
    rhs_base = storage * pressure - combined + gravity
    total_mob = weights[0] * mobility[0] + weights[1] * mobility[1] + weights[2] * mobility[2]
    owned_count = well_mode.shape[0]
    wells_count = owned_count * lax.axis_size("gx") * lax.axis_size("gy")
    cell_count = total_mob.size
    perf_slots = perf_cell[0]
    is_live = perf_well[0] >= 0
    well_ids = jnp.where(is_live, perf_well[0], 0)
    perf_factor = jnp.where(is_live, perf_index[0] * total_mob.reshape(-1)[perf_slots], 0.0)
    well_base = jax.ops.segment_sum(perf_factor, well_ids, num_segments=wells_count)
    well_diag = (
        jnp.zeros((cell_count,), jnp.float32)
        .at[perf_slots]
        .add(perf_factor)
        .reshape(pressure.shape)
    )
    total_diag = storage + faces_total + well_diag
    current = pressure
    well_bhp = well_target
    for sweep_index in range(SWEEPS):
        if sweep_index == 0:
            areal_besides = first_besides
        else:
            rim_current = extended(current, (("gx", 1), ("gy", 2)), 1)
            areal_besides = plus_minus(rim_current, 0) + plus_minus(rim_current, 1)
        at_perf = current.reshape(-1)[perf_slots]
        well_part = jax.ops.segment_sum(perf_factor * at_perf, well_ids, num_segments=wells_count)
        if sweep_index == 0:
            partial_value = jnp.stack((well_part, well_base))
        else:
            partial_value = well_part[None]
        reduced = lax.psum_scatter(partial_value, ("gx", "gy"), scatter_dimension=1, tiled=True)
        if sweep_index == 0:
            owned_base = reduced[1]
        well_bhp = jnp.where(well_mode == 0, well_target, (reduced[0] - well_target) / owned_base)
        every_bhp = lax.all_gather(well_bhp, ("gx", "gy"), axis=0, tiled=True)
        well_rhs = (
            jnp.zeros((cell_count,), jnp.float32)
            .at[perf_slots]
            .add(perf_factor * every_bhp[well_ids])
            .reshape(pressure.shape)
        )
        besides = areal_besides + (neighbour(current, 0, 1), neighbour(current, 0, -1))
        current = (
            current
            + RELAXATION
            * (rhs_base + well_rhs - total_diag * current + coupled_sum(couplings, besides))
            / total_diag
        )
    return (current, well_bhp)


def solution(mesh):
    return jax.shard_map(
        body,
        mesh=mesh,
        in_specs=(
            P(None, "gx", "gy"),
            P(None, None, "gx", "gy"),
            P(None, None, "gx", "gy"),
            P(None, "gx", "gy"),
            P(None, "gx", "gy"),
            P(None, None, "gx", "gy"),
            P(None, "gx", "gy"),
            P(("gx", "gy"), None),
            P(("gx", "gy"), None),
            P(("gx", "gy"), None),
            P(("gx", "gy")),
            P(("gx", "gy")),
        ),
        out_specs=(P(None, "gx", "gy"), P(("gx", "gy"))),
        check_vma=False,
    )
```

profile of v0, /device:TPU:1, one launch (start us, length us, event | category | flops | bytes accessed | tf_op | source)
XLA Modules:
  0.0 1544.0 jit_solution(6372318417789482969)
XLA Ops:
  7.3 2.1 multiply_add_fusion
  10.1 4.4 collective-permute-start
  14.4 1.3 collective-permute-start.1
  17.0 6.2 gather_fusion
  23.2 6.2 gather_fusion.1
  29.4 7.5 scatter_custom_fusion.1
  36.9 7.5 scatter_custom_fusion
  44.5 2.0 copy.57
  48.4 1.9 fusion.122
  50.3 2.3 copy.53
  52.6 4.0 collective-permute-start.2
  57.4 1.9 collective-permute-start.3
  59.4 6.7 scatter_custom_fusion.3
  66.9 2.1 copy.56
  68.9 4.0 pad_maximum_fusion
  74.2 615.7 %reduce-scatter.7.cloned.1.call-done = f32[32,2]{1,0:T(8,128)} async-done(((f32[4096,2]{1,0:T(8,128)}), f32[32,2]{1,0:T(8,128)}) %reduce-scatter.7.cloned.1.call-update) | async-done | bytes 272
  691.5 69.4 %all-reduce.8 = f32[4096]{0:T(1024)S(1)} all-reduce(f32[4096]{0:T(1024)S(1)} %fusion.116), channel_id=1, replica_groups=mesh['gx'=16,'gy'=8] {'gx','gy'}, use_global_device_ids=true, to_apply=%add.8 | all-reduce | flops 4096 | bytes 32768
  760.9 6.1 gather_fusion.2
  767.0 6.7 scatter_custom_fusion.2
  773.7 6.3 fusion.32
  781.9 4.6 collective-permute-start.5
  786.5 6.1 gather_fusion.3
  793.3 7.5 scatter_custom_fusion.4
  800.8 2.0 copy.59
  804.4 3.4 collective-permute-start.6
  807.8 2.2 collective-permute-start.7
  810.0 631.0 %reduce-scatter.9.cloned.1.call-done = f32[32,1]{1,0:T(8,128)} async-done(((f32[4096,1]{1,0:T(8,128)}), f32[32,1]{1,0:T(8,128)}) %reduce-scatter.9.cloned.1.call-update) | async-done | bytes 144
  1441.0 1.4 copy.60
  1444.1 69.2 %all-reduce.9 = f32[4096]{0:T(1024)S(1)} all-reduce(f32[4096]{0:T(1024)} %copy-done.9), channel_id=1, replica_groups=mesh['gx'=16,'gy'=8] {'gx','gy'}, use_global_device_ids=true, to_apply=%add.9 | all-reduce | flops 4096 | bytes 32768
  1513.3 10.6 gather_fusion.4
  1524.6 6.7 scatter_custom_fusion.5
  1531.3 5.8 fusion.40
  (85 shorter events, 14.9 us)
Async XLA Ops:
  7.2 2.2 copy-start
  7.2 2.2 copy-start.2
  7.2 2.3 copy-start.3
  7.2 2.4 copy-start.4
  7.2 682.7 %reduce-scatter.7.cloned.1.call-start = ((), (), s32[]{:S(2)}) async-start(), calls=%async_computation.2 | async-start | bytes 2113536
  7.3 2.3 copy-start.7
  9.3 0.7 copy-start.6
  9.3 13.8 copy-start.5
  9.3 6.4 copy-start.11
  9.3 7.6 copy-start.14
  10.0 38.1 %copy-start.1 = (f32[8,12,32,128]{3,2,1,0:T(8,128)}, f32[8,12,32,128]{3,2,1,0:T(8,128)S(1)}, u32[]{:S(2)}) copy-start(f32[8,12,32,128]{3,2,1,0:T(8,128)S(1)} %bitcast_dynamic-update-slice_fusion) | copy-start | bytes 4718596
  10.1 38.0 %collective-permute-start = (f32[8,12,1,128]{3,2,1,0:T(1,128)S(1)}, f32[8,12,1,128]{3,2,1,0:T(1,128)S(1)}, u32[]{:S(2)}, u32[]{:S(2)}) collective-permute-start(f32[8,12,1,128]{3,2,1,0:T(1,128)S(1)} %get-tuple-element.26), channel_id=1, source_target_pairs={{0,8},{8,16},{16,24},{24,32},{32,40},{40,48},{48,56},{56,64},{64,7... | collective-permute-start | bytes 147464 | tf_op jit(solution)/shard_map/ppermute | solution.py:28
  14.4 33.7 %collective-permute-start.1 = (f32[8,12,1,128]{3,2,1,0:T(1,128)S(1)}, f32[8,12,1,128]{3,2,1,0:T(1,128)S(1)}, u32[]{:S(2)}, u32[]{:S(2)}) collective-permute-start(f32[8,12,1,128]{3,2,1,0:T(1,128)S(1)} %get-tuple-element.27), channel_id=1, source_target_pairs={{8,0},{16,8},{24,16},{32,24},{40,32},{48,40},{56,48},{64,56},{72,6... | collective-permute-start | bytes 147464 | tf_op jit(solution)/shard_map/ppermute | solution.py:30
  17.0 6.2 copy-start.12
  23.2 6.2 copy-start.15
  23.2 6.2 copy-start.16
  29.4 763.3 %copy-start.8 = (f32[1024]{0:T(1024)}, f32[1024]{0:T(1024)S(1)}, u32[]{:S(2)}) copy-start(f32[1024]{0:T(1024)S(1)} %get-tuple-element.12) | copy-start | bytes 12292
  46.5 1394.5 %reduce-scatter.9.cloned.1.call-start = ((), (), s32[]{:S(2)}) async-start(), calls=%async_computation.3 | async-start | bytes 2113536
  52.6 13.4 collective-permute-start.2
  57.4 9.5 collective-permute-start.3
  59.4 701.5 %copy-start.10 = (s32[1024]{0:T(1024)}, s32[1024]{0:T(1024)S(1)}, u32[]{:S(2)}) copy-start(s32[1024]{0:T(1024)S(1)} %broadcast_clamp_fusion) | copy-start | bytes 12292
  73.0 618.0 %copy-start.17 = (f32[32]{0:T(128)S(1)}, f32[32]{0:T(128)}, u32[]{:S(2)}) copy-start(f32[32]{0:T(128)} %param.23) | copy-start | bytes 388
  73.0 618.0 %copy-start.18 = (s32[32]{0:T(128)S(1)}, s32[32]{0:T(128)}, u32[]{:S(2)}) copy-start(s32[32]{0:T(128)} %param.22) | copy-start | bytes 388
  690.9 0.6 copy-start.13
  780.6 22.2 %collective-permute-start.4 = (f32[12,1,128]{2,1,0:T(1,128)}, f32[12,1,128]{2,1,0:T(1,128)}, u32[]{:S(2)}, u32[]{:S(2)}) collective-permute-start(f32[12,1,128]{2,1,0:T(1,128)} %get-tuple-element.32), channel_id=1, source_target_pairs={{8,0},{16,8},{24,16},{32,24},{40,32},{48,40},{56,48},{64,56},{72,6... | collective-permute-start | bytes 18440 | tf_op jit(solution)/shard_map/ppermute | solution.py:30
  781.9 20.9 %collective-permute-start.5 = (f32[12,1,128]{2,1,0:T(1,128)}, f32[12,1,128]{2,1,0:T(1,128)}, u32[]{:S(2)}, u32[]{:S(2)}) collective-permute-start(f32[12,1,128]{2,1,0:T(1,128)} %get-tuple-element.31), channel_id=1, source_target_pairs={{0,8},{8,16},{16,24},{24,32},{32,40},{40,48},{48,56},{56,64},{64,7... | collective-permute-start | bytes 18440 | tf_op jit(solution)/shard_map/ppermute | solution.py:28
  804.4 726.8 %collective-permute-start.6 = (f32[12,34,1]{2,1,0:T(8,128)}, f32[12,34,1]{2,1,0:T(8,128)}, u32[]{:S(2)}, u32[]{:S(2)}) collective-permute-start(f32[12,34,1]{2,1,0:T(8,128)} %get-tuple-element.29), channel_id=1, source_target_pairs={{1,0},{2,1},{3,2},{4,3},{5,4},{6,5},{7,6},{9,8},{10,9},{11,10},{12... | collective-permute-start | bytes 4904 | tf_op jit(solution)/shard_map/ppermute | solution.py:30
  807.8 723.5 %collective-permute-start.7 = (f32[12,34,1]{2,1,0:T(8,128)}, f32[12,34,1]{2,1,0:T(8,128)}, u32[]{:S(2)}, u32[]{:S(2)}) collective-permute-start(f32[12,34,1]{2,1,0:T(8,128)} %get-tuple-element.30), channel_id=1, source_target_pairs={{0,1},{1,2},{2,3},{3,4},{4,5},{5,6},{6,7},{8,9},{9,10},{10,11},{11... | collective-permute-start | bytes 4904 | tf_op jit(solution)/shard_map/ppermute | solution.py:28
  1443.5 0.6 copy-start.9
Sparse Core Ops, SparseCore 0:
  46.6 643.3 reduce-scatter.6
  802.9 637.9 reduce-scatter.8
where the time goes:
time: 1550 us; the launch traced here: 1540 us
  waiting for transfers between devices  1250 us (81%)
  blocking collectives  139 us (9%)
  other arithmetic  66.7 us (4%)
  local copies, waits for them, and re-layouts  54.4 us (4%)
  starting transfers between devices  23.1 us (1%)
    unnamed x4, waiting for transfers between devices  1250 us
    unnamed x2, blocking collectives  139 us
  transfers between devices with their start and end apart: 10, of which 2 were waited for; matrix products, arithmetic and copies ran while one was open for 6% of the time, Pallas kernels for 0%

commit v1 on v0

v1 whole, which is shorter than its diff:
```python
import jax
import jax.numpy as jnp
from jax import lax
from jax.experimental import pallas as pl
from jax.experimental.pallas import tpu as pltpu
from jax.sharding import PartitionSpec as P

MESH = pl.DeviceIdType.MESH
NZ, CX, CY = 12, 32, 128
ROWS = NZ * CX
SLOTS = 1024
NGX, NGY = 16, 8
GAMMA = (0.4, 0.5, 0.08)
F32, BF16 = jnp.float32, jnp.bfloat16
CONTRACT_LAST = (((1,), (1,)), ((), ()))
CONTRACT_FIRST = (((0,), (0,)), ((), ()))


def split(x):
    high = x.astype(BF16)
    return high, (x - high.astype(F32)).astype(BF16)


def phase_state(p, sw, sg):
    so = 1.0 - sw - sg
    bo = 1.0 + 0.2 * (p - 1.0)
    bw = 1.0 + 0.05 * (p - 1.0)
    return so, bo, bw


def kernel(
    p_ref, sat_ref, perm_ref, pv_ref, dep_ref, res_ref, flag_ref, pc_ref, pw_ref, pi_ref, wm_ref, wt_ref,
    out_ref, bhp_ref,
    mob, onehot, fields, spread, wrow, coup, pre, inv, rhs, cur, wacc, slotv,
    table, rs_recv, xs_src, xs_recv, tm_src, tm_recv, ball,
    hx_send, hx_recv, hy_send, hy_recv, halo_y, hx2_send, hx2_recv, hy2_send, hy2_recv,
    rs_ss, rs_rs, xs_ss, xs_rs, tm_ss, tm_rs, bh_ss, bh_rs, h_ss, h_rs,
):
    ix, iy = lax.axis_index("gx"), lax.axis_index("gy")

    def gx_peer(k):
        return (lax.rem(ix + k, NGX), iy)

    def gy_peer(k):
        return (ix, lax.rem(iy + k, NGY))

    barrier = pltpu.get_barrier_semaphore()

    @pl.loop(1, NGX)
    def _(k):
        pl.semaphore_signal(barrier, inc=1, device_id=gx_peer(k), device_id_type=MESH)

    @pl.loop(1, NGY)
    def _(k):
        pl.semaphore_signal(barrier, inc=1, device_id=gy_peer(k), device_id_type=MESH)

    lane = lax.broadcasted_iota(jnp.int32, (CX, CY), 1)
    row = lax.broadcasted_iota(jnp.int32, (CX, CY), 0)

    def rs_copy(t, k):
        return pltpu.make_async_remote_copy(
            src_ref=table.at[t, lax.rem(iy + k, NGY)], dst_ref=rs_recv.at[t, k - 1],
            send_sem=rs_ss.at[t, k - 1], recv_sem=rs_rs.at[t, k - 1],
            device_id=gy_peer(k), device_id_type=MESH)

    def xs_copy(t, k):
        return pltpu.make_async_remote_copy(
            src_ref=xs_src.at[t], dst_ref=xs_recv.at[t, k - 1],
            send_sem=xs_ss.at[t, k - 1], recv_sem=xs_rs.at[t, k - 1],
            device_id=gx_peer(k), device_id_type=MESH)

    def tm_copy(k):
        return pltpu.make_async_remote_copy(
            src_ref=tm_src, dst_ref=tm_recv.at[k - 1],
            send_sem=tm_ss.at[k - 1], recv_sem=tm_rs.at[k - 1],
            device_id=gx_peer(k), device_id_type=MESH)

    def bh_send(t, k):
        return pltpu.make_async_remote_copy(
            src_ref=ball.at[t, iy], dst_ref=ball.at[t, iy],
            send_sem=bh_ss.at[t, k - 1], recv_sem=bh_rs.at[t, k - 1],
            device_id=gy_peer(k), device_id_type=MESH)

    def bh_recv(t, k):
        other = lax.rem(iy + NGY - k, NGY)
        return pltpu.make_async_remote_copy(
            src_ref=ball.at[t, other], dst_ref=ball.at[t, other],
            send_sem=bh_ss.at[t, k - 1], recv_sem=bh_rs.at[t, k - 1],
            device_id=gy_peer(k), device_id_type=MESH)

    def halo_copies(xs, xr, ys, yr, base):
        def one(src, dst, n, dev):
            return pltpu.make_async_remote_copy(
                src_ref=src, dst_ref=dst, send_sem=h_ss.at[base + n], recv_sem=h_rs.at[base + n],
                device_id=dev, device_id_type=MESH)
        return (
            one(xs.at[1], xr.at[0], 0, gx_peer(1)),
            one(xs.at[0], xr.at[1], 1, gx_peer(NGX - 1)),
            one(ys.at[1], yr.at[0], 2, gy_peer(1)),
            one(ys.at[0], yr.at[1], 3, gy_peer(NGY - 1)),
        )

    halo1 = halo_copies(hx_send, hx_recv, hy_send, hy_recv, 0)
    halo2 = halo_copies(hx2_send, hx2_recv, hy2_send, hy2_recv, 4)

    @pl.loop(0, NZ)
    def _(z):
        p, sw, sg = p_ref[z], sat_ref[0, z], sat_ref[1, z]
        so, bo, bw = phase_state(p, sw, sg)
        so2, sw2, sg2 = so * so * 0.5, sw * sw, sg * sg * 5.0
        m = (so2 * bo, sw2 * bw, sg2 * p)
        for c in range(3):
            mob[c, z] = m[c]
        total = so2 + sw2 + sg2
        rows = pl.ds(pl.multiple_of(z * CX, CX), CX)
        for n, part in enumerate(split(total) + split(p)):
            fields[rows, n * CY:(n + 1) * CY] = part
        flags = flag_ref[z]
        bit_x = (flags & 1).astype(F32)
        bit_y = ((flags >> 1) & 1).astype(F32)
        dep = dep_ref[z]
        xf = m + (perm_ref[0, z], dep, bit_x, p)
        yf = m + (perm_ref[1, z], dep, bit_y, p)
        for n, f in enumerate(xf):
            hx_send[0, z, n:n + 1, :] = f[0:1, :]
            hx_send[1, z, n:n + 1, :] = f[CX - 1:CX, :]
        hx_send[0, z, 7:8, :] = jnp.zeros((1, CY), F32)
        hx_send[1, z, 7:8, :] = jnp.zeros((1, CY), F32)
        packed = jnp.zeros((CX, CY), F32)
        for n, f in enumerate(yf):
            packed = jnp.where(lane == n, pltpu.roll(f, (n + 1) % CY, 1), packed)
            packed = jnp.where(lane == 8 + n, pltpu.roll(f, 8 + n, 1), packed)
        halo_y[z] = packed

    cell = pc_ref[...]
    cell_row, cell_lane = cell >> 7, cell & 127
    live = pw_ref[...] >= 0
    well = jnp.where(live, pw_ref[...], 0)
    well_row = ((well >> 5) & 7) * 8 + (well >> 10)
    well_lane = ((well >> 8) & 3) * 32 + (well & 31)
    slotv[0:1, :] = jnp.where(live, pi_ref[...], 0.0)

    @pl.loop(0, NZ)
    def _(z):
        ids = lax.broadcasted_iota(jnp.int32, (CX, SLOTS), 0) + z * CX
        onehot[pl.ds(pl.multiple_of(z * CX, CX), CX), :] = jnp.where(ids == cell_row, 1.0, 0.0).astype(BF16)

    well_ids = lax.broadcasted_iota(jnp.int32, (64, SLOTS), 0)
    wrow[0:64, :] = jnp.where(well_ids == well_row, 1.0, 0.0).astype(BF16)
    wrow[64:128, :] = jnp.where(well_ids == well_row + 4, 1.0, 0.0).astype(BF16)

    sub256 = lax.broadcasted_iota(jnp.int32, (CY, 256), 0)

    def lane_rows(ref_row, chunk):
        if ref_row == 0:
            ids = pc_ref[0:1, chunk] & 127
        else:
            w = jnp.maximum(pw_ref[0:1, chunk], 0)
            ids = ((w >> 8) & 3) * 32 + (w & 31)
        return ids

    def picked(operand, rows_ref, which, count, dst):
        @pl.loop(0, SLOTS // 256)
        def _(j):
            chunk = pl.ds(pl.multiple_of(j * 256, 256), 256)
            g = lax.dot_general(operand, rows_ref[0:operand.shape[0], chunk], CONTRACT_FIRST, preferred_element_type=F32)
            mask = sub256 == lane_rows(which, chunk)
            for n in range(count):
                both = g[2 * n * CY:(2 * n + 1) * CY] + g[(2 * n + 1) * CY:(2 * n + 2) * CY]
                slotv[dst + n:dst + n + 1, chunk] = jnp.sum(jnp.where(mask, both, 0.0), axis=0, keepdims=True)

    def spread_lanes(value_row, which, base):
        @pl.loop(0, SLOTS // 256)
        def _(j):
            chunk = pl.ds(pl.multiple_of(j * 256, 256), 256)
            v = jnp.where(sub256 == lane_rows(which, chunk), slotv[value_row:value_row + 1, chunk], 0.0)
            high, low = split(v)
            spread[base:base + CY, chunk] = high
            spread[base + CY:base + 2 * CY, chunk] = low

    def scatter_cells(value_row):
        spread_lanes(value_row, 0, 0)
        both = lax.dot_general(onehot[...], spread[0:256, :], CONTRACT_LAST, preferred_element_type=F32)
        wacc[...] = both[:, 0:CY] + both[:, CY:2 * CY]

    def well_sums(value_row, with_base):
        spread_lanes(value_row, 1, 0)
        both = lax.dot_general(wrow[0:64, :], spread[0:256, :], CONTRACT_LAST, preferred_element_type=F32)
        if with_base:
            spread_lanes(1, 1, 256)
            both = both + lax.dot_general(wrow[64:128, :], spread[256:512, :], CONTRACT_LAST, preferred_element_type=F32)
        sums = both[:, 0:CY] + both[:, CY:2 * CY]
        return sums.reshape(NGY, 8, CY)

    picked(fields[...], onehot, 0, 2, 4)
    factor = slotv[0:1, :] * slotv[4:5, :]
    slotv[1:2, :] = factor
    slotv[2:3, :] = factor * slotv[5:6, :]
    table[0] = well_sums(2, True)

    quarter = lax.broadcasted_iota(jnp.int32, (8, CY), 1) // 32
    line = lax.broadcasted_iota(jnp.int32, (8, CY), 0)
    own = (quarter == lax.rem(ix, 4)) & (line % 4 == ix // 4)
    target4 = jnp.concatenate([wt_ref[...]] * 4, axis=1)
    mode4 = jnp.concatenate([wm_ref[...].astype(F32)] * 4, axis=1)
    controls = jnp.where(line < 4, jnp.broadcast_to(target4, (8, CY)), jnp.broadcast_to(mode4, (8, CY)))
    tm_src[...] = jnp.where(own, controls, 0.0)

    pl.semaphore_wait(barrier, NGX + NGY - 2)

    def send_table(t):
        @pl.loop(1, NGY)
        def _(k):
            rs_copy(t, k).start()

    def exchange(t):
        @pl.loop(1, NGY)
        def _(k):
            rs_copy(t, k).wait_recv()
        part = table[t, iy]
        for k in range(NGY - 1):
            part = part + rs_recv[t, k]
        xs_src[t] = part

        @pl.loop(1, NGX)
        def _(k):
            xs_copy(t, k).start()

    def finish_sums(t):
        @pl.loop(1, NGX)
        def _(k):
            xs_copy(t, k).wait_recv()
        total = xs_src[t]
        for k in range(NGX - 1):
            total = total + xs_recv[t, k]
        return total

    def share_bhp(t, value):
        ball[t, iy] = value

        @pl.loop(1, NGY)
        def _(k):
            bh_send(t, k).start()

        @pl.loop(1, NGY)
        def _(k):
            bh_recv(t, k).wait_recv()

    send_table(0)

    @pl.loop(1, NGX)
    def _(k):
        tm_copy(k).start()

    turned = halo_y[...].reshape(ROWS, CY).T
    hy_send[1] = turned[0:8, :]
    hy_send[0] = turned[8:16, :]
    for copy in halo1:
        copy.start()

    exchange(0)

    scatter_cells(1)
    for copy in halo1:
        copy.wait_recv()
    stacked = jnp.concatenate([hy_recv[0], hy_recv[1], jnp.zeros((CY - 16, ROWS), F32)], axis=0)
    halo_y[...] = stacked.T.reshape(NZ, CX, CY)

    def face(w, m, n, k, kn, up, drop):
        trans = 2.0 * k * kn / (k + kn)
        c = jnp.zeros((CX, CY), F32)
        g = jnp.zeros((CX, CY), F32)
        for i in range(3):
            flux = w[i] * jnp.where(up, m[i], n[i])
            c = c + flux
            g = g + GAMMA[i] * flux
        c = c * trans
        return c, g * (trans * drop)

    @pl.loop(0, NZ)
    def _(z):
        p, sw, sg = p_ref[z], sat_ref[0, z], sat_ref[1, z]
        so, bo, bw = phase_state(p, sw, sg)
        w = (1.0 / bo, 1.0 / bw, 1.0 / p)
        m = (mob[0, z], mob[1, z], mob[2, z])
        dep = dep_ref[z]
        flags = flag_ref[z]
        storage = pv_ref[z] * (so * 0.2 * w[0] + sw * 0.05 * w[1] + sg * w[2])
        lift = jnp.zeros((CX, CY), F32)
        faces = jnp.zeros((CX, CY), F32)
        beside = jnp.zeros((CX, CY), F32)

        def add(n, lift, faces, beside, c, g, pn):
            coup[n, z] = c
            return lift + g, faces + c, beside + c * pn

        for side in range(2):
            halo = hx_recv[side, z]
            edge = 0 if side == 0 else CX - 1
            inside = (ix > 0) if side == 0 else (ix < NGX - 1)

            def shifted(f, n):
                return jnp.where(row == edge, jnp.broadcast_to(halo[n:n + 1, :], (CX, CY)), pltpu.roll(f, 1 if side == 0 else CX - 1, 0))
            k = perm_ref[0, z]
            kn = shifted(k, 3)
            kn = jnp.where((row == edge) & jnp.logical_not(inside), 0.0, kn)
            if side == 0:
                up = shifted((flags & 1).astype(F32), 5) < 0.5
            else:
                up = (flags & 1) == 1
            c, g = face(w, m, tuple(shifted(m[i], i) for i in range(3)), k, kn, up, dep - shifted(dep, 4))
            lift, faces, beside = add(side, lift, faces, beside, c, g, shifted(p, 6))

        pack = halo_y[z]
        for side in range(2):
            edge = 0 if side == 0 else CY - 1
            inside = (iy > 0) if side == 0 else (iy < NGY - 1)

            def shifted(f, n):
                moved = pltpu.roll(pack, (CY - n) % CY if side == 0 else CY - 1 - 8 - n, 1)
                return jnp.where(lane == edge, moved, pltpu.roll(f, 1 if side == 0 else CY - 1, 1))
            k = perm_ref[1, z]
            kn = shifted(k, 3)
            kn = jnp.where((lane == edge) & jnp.logical_not(inside), 0.0, kn)
            if side == 0:
                up = shifted(((flags >> 1) & 1).astype(F32), 5) < 0.5
            else:
                up = ((flags >> 1) & 1) == 1
            c, g = face(w, m, tuple(shifted(m[i], i) for i in range(3)), k, kn, up, dep - shifted(dep, 4))
            lift, faces, beside = add(2 + side, lift, faces, beside, c, g, shifted(p, 6))

        for side in range(2):
            zn = jnp.maximum(z - 1, 0) if side == 0 else jnp.minimum(z + 1, NZ - 1)
            inside = (z > 0) if side == 0 else (z < NZ - 1)
            k = perm_ref[2, z]
            kn = jnp.where(inside, perm_ref[2, zn], 0.0)
            if side == 0:
                up = (flag_ref[zn] >> 2) == 0
            else:
                up = (flags >> 2) == 1
            c, g = face(w, m, (mob[0, zn], mob[1, zn], mob[2, zn]), k, kn, up, dep - dep_ref[zn])
            lift, faces, beside = add(4 + side, lift, faces, beside, c, g, p_ref[zn])

        combined = w[0] * res_ref[0, z] + w[1] * res_ref[1, z] + w[2] * res_ref[2, z]
        b = storage * p - combined + lift
        rows = pl.ds(pl.multiple_of(z * CX, CX), CX)
        damp = 0.8 / (storage + faces + wacc[rows, :])
        rhs[z] = b
        inv[z] = damp
        pre[z] = 0.2 * p + damp * (b + beside)

    @pl.loop(1, NGX)
    def _(k):
        tm_copy(k).wait_recv()
    controls = tm_src[...]
    for k in range(NGX - 1):
        controls = controls + tm_recv[k]
    mode = pltpu.roll(controls, 4, 0)

    def bhp_of(sums, base):
        value = jnp.where(mode < 0.5, controls, (sums - controls) / base)
        return jnp.where(line < 4, value, 0.0)

    def apply_bhp(t):
        wells = ball[t].reshape(64, CY)
        high, low = split(wells)
        picked(jnp.concatenate([high, low], axis=1), wrow, 1, 1, 3)
        slotv[2:3, :] = slotv[1:2, :] * slotv[3:4, :]
        scatter_cells(2)

    sums = finish_sums(0)
    base = pltpu.roll(sums, 4, 0)
    share_bhp(0, bhp_of(sums, base))
    apply_bhp(0)

    @pl.loop(0, NZ)
    def _(z):
        rows = pl.ds(pl.multiple_of(z * CX, CX), CX)
        c = pre[z] + inv[z] * wacc[rows, :]
        cur[z] = c
        for n, part in enumerate(split(c)):
            fields[rows, n * CY:(n + 1) * CY] = part
        hx2_send[0, z] = c[0:1, :]
        hx2_send[1, z] = c[CX - 1:CX, :]
        packed = jnp.where(lane == 0, pltpu.roll(c, 1, 1), 0.0)
        halo_y[z] = jnp.where(lane == 8, pltpu.roll(c, 8, 1), packed)

    picked(fields[:, 0:256], onehot, 0, 1, 5)
    slotv[2:3, :] = slotv[1:2, :] * slotv[5:6, :]
    table[1] = well_sums(2, False)
    send_table(1)
    turned = halo_y[...].reshape(ROWS, CY).T
    hy2_send[1] = turned[0:8, :]
    hy2_send[0] = turned[8:16, :]
    for copy in halo2:
        copy.start()
    exchange(1)

    for copy in halo2:
        copy.wait_recv()
    stacked = jnp.concatenate([hy2_recv[0], hy2_recv[1], jnp.zeros((CY - 16, ROWS), F32)], axis=0)
    halo_y[...] = stacked.T.reshape(NZ, CX, CY)

    @pl.loop(0, NZ)
    def _(z):
        c = cur[z]
        pack = halo_y[z]
        up_x = jnp.where(row == 0, jnp.broadcast_to(hx2_recv[0, z], (CX, CY)), pltpu.roll(c, 1, 0))
        down_x = jnp.where(row == CX - 1, jnp.broadcast_to(hx2_recv[1, z], (CX, CY)), pltpu.roll(c, CX - 1, 0))
        up_y = jnp.where(lane == 0, pack, pltpu.roll(c, 1, 1))
        down_y = jnp.where(lane == CY - 1, pltpu.roll(pack, CY - 9, 1), pltpu.roll(c, CY - 1, 1))
        up_z, down_z = cur[jnp.maximum(z - 1, 0)], cur[jnp.minimum(z + 1, NZ - 1)]
        total = rhs[z]
        for n, value in enumerate((up_x, down_x, up_y, down_y, up_z, down_z)):
            total = total + coup[n, z] * value
        pre[z] = 0.2 * c + inv[z] * total

    value = bhp_of(finish_sums(1), base)
    share_bhp(1, value)
    apply_bhp(1)

    @pl.loop(0, NZ)
    def _(z):
        rows = pl.ds(pl.multiple_of(z * CX, CX), CX)
        out_ref[z] = pre[z] + inv[z] * wacc[rows, :]

    mine = jnp.sum(jnp.where(own & (line < 4), value, 0.0), axis=0, keepdims=True)
    mine = jnp.broadcast_to(mine, (8, CY))
    mine = mine + pltpu.roll(mine, 32, 1) + pltpu.roll(mine, 64, 1) + pltpu.roll(mine, 96, 1)
    bhp_ref[...] = mine[0:1, 0:32]

    for t in range(2):
        @pl.loop(1, NGY)
        def _(k):
            rs_copy(t, k).wait_send()
            bh_send(t, k).wait_send()

        @pl.loop(1, NGX)
        def _(k):
            xs_copy(t, k).wait_send()

    @pl.loop(1, NGX)
    def _(k):
        tm_copy(k).wait_send()
    for copy in halo1 + halo2:
        copy.wait_send()


def body(pressure, saturation, permeability, pore_volume, cell_depth, residual, upstream_flags,
         perf_cell, perf_well, perf_index, well_mode, well_target):
    grid = (NZ, CX, CY)
    vmem = pl.BlockSpec(memory_space=pltpu.VMEM)
    dma = pltpu.SemaphoreType.DMA
    new_pressure, well_bhp = pl.pallas_call(
        kernel,
        out_shape=(jax.ShapeDtypeStruct(grid, F32), jax.ShapeDtypeStruct((1, 32), F32)),
        in_specs=[vmem] * 12,
        out_specs=(vmem, vmem),
        scratch_shapes=[
            pltpu.VMEM((3,) + grid, F32),
            pltpu.VMEM((ROWS, SLOTS), BF16),
            pltpu.VMEM((ROWS, 4 * CY), BF16),
            pltpu.VMEM((4 * CY, SLOTS), BF16),
            pltpu.VMEM((128, SLOTS), BF16),
            pltpu.VMEM((6,) + grid, F32),
            pltpu.VMEM(grid, F32),
            pltpu.VMEM(grid, F32),
            pltpu.VMEM(grid, F32),
            pltpu.VMEM(grid, F32),
            pltpu.VMEM((ROWS, CY), F32),
            pltpu.VMEM((8, SLOTS), F32),
            pltpu.VMEM((2, NGY, 8, CY), F32),
            pltpu.VMEM((2, NGY - 1, 8, CY), F32),
            pltpu.VMEM((2, 8, CY), F32),
            pltpu.VMEM((2, NGX - 1, 8, CY), F32),
            pltpu.VMEM((8, CY), F32),
            pltpu.VMEM((NGX - 1, 8, CY), F32),
            pltpu.VMEM((2, NGY, 8, CY), F32),
            pltpu.VMEM((2, NZ, 8, CY), F32),
            pltpu.VMEM((2, NZ, 8, CY), F32),
            pltpu.VMEM((2, 8, ROWS), F32),
            pltpu.VMEM((2, 8, ROWS), F32),
            pltpu.VMEM(grid, F32),
            pltpu.VMEM((2, NZ, 1, CY), F32),
            pltpu.VMEM((2, NZ, 1, CY), F32),
            pltpu.VMEM((2, 8, ROWS), F32),
            pltpu.VMEM((2, 8, ROWS), F32),
            dma((2, NGY - 1)), dma((2, NGY - 1)),
            dma((2, NGX - 1)), dma((2, NGX - 1)),
            dma((NGX - 1,)), dma((NGX - 1,)),
            dma((2, NGY - 1)), dma((2, NGY - 1)),
            dma((8,)), dma((8,)),
        ],
        compiler_params=pltpu.CompilerParams(collective_id=0, has_side_effects=True),
        name="cpr_step",
    )(pressure, saturation, permeability, pore_volume, cell_depth, residual, upstream_flags,
      perf_cell, perf_well, perf_index, well_mode.reshape(1, 32), well_target.reshape(1, 32))
    return new_pressure, well_bhp.reshape(32)


def solution(mesh):
    areal, stacked, owned = P(None, "gx", "gy"), P(None, None, "gx", "gy"), P(("gx", "gy"))
    slots = P(("gx", "gy"), None)
    return jax.shard_map(
        body,
        mesh=mesh,
        in_specs=(areal, stacked, stacked, areal, areal, stacked, areal, slots, slots, slots, owned, owned),
        out_specs=(areal, owned),
        check_vma=False,
    )
```

time: 1550 us -> 45.2 us (0.03)
  waiting for transfers between devices: 1250 us -> 0 us
  blocking collectives: 139 us -> 0 us
  other arithmetic: 66.7 us -> 0 us
  local copies, waits for them, and re-layouts: 54.4 us -> 2.13 us
  Pallas kernels: 0 us -> 42.2 us
  starting transfers between devices: 23.1 us -> 0 us
    unnamed x4 -> x0, waiting for transfers between devices: 1250 us -> none
    unnamed x2 -> x0, blocking collectives: 139 us -> none
    scatter-add x6 -> x0, other arithmetic: 42.6 us -> none  [the longest x2 15 us: body(): jax.ops.segment_sum(perf_factor * at_perf, well_ids, num_segments=wells_c...]
    pallas_call x0 -> x1, Pallas kernels: none -> 42.2 us  [body(): pl.pallas_call(kernel, out_shape=(jax.ShapeDtypeStruct(grid, F32), jax.Sh...]
    gather x5 -> x0, local copies, waits for them, and re-layouts: 35.2 us -> none  [the longest x2 16.7 us: body(): every_bhp[well_ids]]
    ppermute x8 -> x0, starting transfers between devices: 23 us -> none  [the longest x4 15.1 us: extended(): lax.ppermute(tail, axis, [(i, (i + 1) % count) for i in range(ends)])]
  transfers between devices with their start and end apart: 10 -> 0, of which waited for: 2 -> 0; matrix products, arithmetic and copies ran while one was open for 6% -> 0% of each run, Pallas kernels for 0% -> 0%
where the time goes in v1:
time: 45.2 us; the launch traced here: 45 us
  Pallas kernels  42.2 us (93%)
  local copies, waits for them, and re-layouts  2.13 us (5%)
  between operations  0.65 us (1%)
    pallas_call x1, Pallas kernels, body(): pl.pallas_call(kernel, out_shape=(jax.ShapeDtypeStruct(grid, F32), jax.Sh...  42.2 us
    unnamed x4, local copies, waits for them, and re-layouts  2.13 us

profile of v1, /device:TPU:1, one launch (start us, length us, event | category | flops | bytes accessed | tf_op | source)
XLA Modules:
  0.0 45.0 jit_solution(3607307185569740284)
XLA Ops:
  0.6 42.2 %cpr_step.1 = (f32[12,32,128]{2,1,0:T(8,128)}, f32[1,32]{1,0:T(1,128)}) custom-call(f32[12,32,128]{2,1,0:T(8,128)} %p_ref.1, f32[2,12,32,128]{3,2,1,0:T(8,128)} %sat_ref.1, f32[3,12,32,128]{3,2,1,0:T(8,128)} %perm_ref.1, f32[12,32,128]{2,1,0:T(8,128)} %pv_ref.1, f32[12,32,128]{2,1,0:T(8,128)} %dep_ref.1, f32[3,12,32,128]{3,2,1,0:T(8,128)} %res_ref.1, ...), custom_call_target="tpu_custom_call" | custom-call | tf_op jit(solution)/shard_map/cpr_step/pallas_call | solution.py:454
  42.9 0.0 copy-start
  42.9 1.6 %copy.16 = f32[12,32,128]{2,1,0:T(8,128)} copy(f32[12,32,128]{2,1,0:T(8,128)} %get-tuple-element.8) | data formatting | bytes 393216
  44.5 0.0 copy-done
  44.5 0.5 %copy.17 = f32[32]{0:T(128)} copy(f32[32]{0:T(128)S(1)} %bitcast.5) | data formatting | bytes 256
Async XLA Ops:
  42.9 1.6 %copy-start = (f32[1,32]{1,0:T(1,128)S(1)}, f32[1,32]{1,0:T(1,128)}, u32[]{:S(2)}) copy-start(f32[1,32]{1,0:T(1,128)} %get-tuple-element.5) | copy-start | bytes 388

commit v2 on v1

v2 whole, which is shorter than its diff:
```python
import jax
import jax.numpy as jnp
from jax import lax
from jax.experimental import pallas as pl
from jax.experimental.pallas import tpu as pltpu
from jax.sharding import PartitionSpec as P

MESH = pl.DeviceIdType.MESH
NZ, CX, CY = 12, 32, 128
ROWS = NZ * CX
SLOTS = 1024
NGX, NGY = 16, 8
GAMMA = (0.4, 0.5, 0.08)
F32, BF16 = jnp.float32, jnp.bfloat16
CONTRACT_LAST = (((1,), (1,)), ((), ()))
CONTRACT_FIRST = (((0,), (0,)), ((), ()))


def split(x):
    high = x.astype(BF16)
    return high, (x - high.astype(F32)).astype(BF16)


def phase_state(p, sw, sg):
    so = 1.0 - sw - sg
    bo = 1.0 + 0.2 * (p - 1.0)
    bw = 1.0 + 0.05 * (p - 1.0)
    return so, bo, bw


def hops(offset, size):
    return min(offset, size - offset)


GX_OFFSETS = sorted(((a, b) for a in range(4) for b in range(4) if a or b), key=lambda o: -hops(o[0], 4) - hops(o[1], 4))
GY_OFFSETS = sorted(((a, b) for a in range(4) for b in range(2) if a or b), key=lambda o: -2 * hops(o[0], 4) - o[1])


def kernel(
    p_hbm, sat_hbm, perm_hbm, pv_hbm, dep_hbm, res_hbm, flag_hbm, pc_hbm, pw_hbm, pi_hbm, wm_hbm, wt_hbm,
    out_ref, bhp_ref,
    p_ref, sat_ref, perm_ref, pv_ref, dep_ref, res_ref, flag_ref, pc_ref, pw_ref, pi_ref, wm_ref, wt_ref,
    mob, onehot, fields, spread, wrow, same, coup, pre, inv, rhs, cur, wacc, slotv,
    table, rs_recv, xs_src, xs_recv, tm_src, tm_recv, ball,
    hx_send, hx_recv, hy_send, hy_recv, halo_y, hx2_send, hx2_recv, hy2_send, hy2_recv,
    in_sem, rs_ss, rs_rs, xs_ss, xs_rs, tm_ss, tm_rs, bh_ss, bh_rs, h_ss, h_rs,
):
    ix, iy = lax.axis_index("gx"), lax.axis_index("gy")
    chip_y, chip_z = ix // 4, lax.rem(ix, 4)
    chip_x, core = iy // 2, lax.rem(iy, 2)

    def gx_of(a, b):
        return lax.rem(chip_y + a, 4) * 4 + lax.rem(chip_z + b, 4)

    def gy_of(a, b):
        return lax.rem(chip_x + a, 4) * 2 + lax.rem(core + b, 2)

    barrier = pltpu.get_barrier_semaphore()
    for a, b in GX_OFFSETS:
        pl.semaphore_signal(barrier, inc=1, device_id=(gx_of(a, b), iy), device_id_type=MESH)
    for a, b in GY_OFFSETS:
        pl.semaphore_signal(barrier, inc=1, device_id=(ix, gy_of(a, b)), device_id_type=MESH)

    loads = {}
    pairs = (("pc", pc_hbm, pc_ref), ("pw", pw_hbm, pw_ref), ("pi", pi_hbm, pi_ref), ("sat", sat_hbm, sat_ref),
             ("p", p_hbm, p_ref), ("perm", perm_hbm, perm_ref), ("dep", dep_hbm, dep_ref), ("flag", flag_hbm, flag_ref),
             ("wm", wm_hbm, wm_ref), ("wt", wt_hbm, wt_ref), ("pv", pv_hbm, pv_ref), ("res", res_hbm, res_ref))
    for n, (name, src, dst) in enumerate(pairs):
        loads[name] = pltpu.make_async_copy(src, dst, in_sem.at[n])
        loads[name].start()

    lane = lax.broadcasted_iota(jnp.int32, (CX, CY), 1)
    row = lax.broadcasted_iota(jnp.int32, (CX, CY), 0)

    def remote(src, dst, ss, rs, dev):
        return pltpu.make_async_remote_copy(src_ref=src, dst_ref=dst, send_sem=ss, recv_sem=rs,
                                            device_id=dev, device_id_type=MESH)

    def rs_copies(t):
        return [remote(table.at[t, gy_of(a, b)], rs_recv.at[t, n], rs_ss.at[t, n], rs_rs.at[t, n], (ix, gy_of(a, b)))
                for n, (a, b) in enumerate(GY_OFFSETS)]

    def xs_copies(t):
        return [remote(xs_src.at[t], xs_recv.at[t, n], xs_ss.at[t, n], xs_rs.at[t, n], (gx_of(a, b), iy))
                for n, (a, b) in enumerate(GX_OFFSETS)]

    tm_copies = [remote(tm_src, tm_recv.at[n], tm_ss.at[n], tm_rs.at[n], (gx_of(a, b), iy))
                 for n, (a, b) in enumerate(GX_OFFSETS)]

    def bh_sends(t):
        return [remote(ball.at[t, iy], ball.at[t, iy], bh_ss.at[t, n], bh_rs.at[t, n], (ix, gy_of(a, b)))
                for n, (a, b) in enumerate(GY_OFFSETS)]

    def bh_recvs(t):
        return [remote(ball.at[t, gy_of((4 - a) % 4, b)], ball.at[t, gy_of((4 - a) % 4, b)], bh_ss.at[t, n], bh_rs.at[t, n],
                       (ix, gy_of(a, b)))
                for n, (a, b) in enumerate(GY_OFFSETS)]

    def halo_copies(xs, xr, ys, yr, base):
        return (
            remote(xs.at[1], xr.at[0], h_ss.at[base], h_rs.at[base], (lax.rem(ix + 1, NGX), iy)),
            remote(xs.at[0], xr.at[1], h_ss.at[base + 1], h_rs.at[base + 1], (lax.rem(ix + NGX - 1, NGX), iy)),
            remote(ys.at[1], yr.at[0], h_ss.at[base + 2], h_rs.at[base + 2], (ix, lax.rem(iy + 1, NGY))),
            remote(ys.at[0], yr.at[1], h_ss.at[base + 3], h_rs.at[base + 3], (ix, lax.rem(iy + NGY - 1, NGY))),
        )

    halo1 = halo_copies(hx_send, hx_recv, hy_send, hy_recv, 0)
    halo2 = halo_copies(hx2_send, hx2_recv, hy2_send, hy2_recv, 4)

    for name in ("pc", "pw", "pi"):
        loads[name].wait()
    cell = pc_ref[...]
    cell_row = cell >> 7
    live = pw_ref[...] >= 0
    well = jnp.where(live, pw_ref[...], 0)
    well_row = ((well >> 5) & 7) * 8 + (well >> 10)
    slotv[0:1, :] = jnp.where(live, pi_ref[...], 0.0)

    @pl.loop(0, NZ)
    def _(z):
        ids = lax.broadcasted_iota(jnp.int32, (CX, SLOTS), 0) + z * CX
        onehot[pl.ds(pl.multiple_of(z * CX, CX), CX), :] = jnp.where(ids == cell_row, 1.0, 0.0).astype(BF16)

    well_ids = lax.broadcasted_iota(jnp.int32, (64, SLOTS), 0)
    wrow[0:64, :] = jnp.where(well_ids == well_row, 1.0, 0.0).astype(BF16)
    wrow[64:128, :] = jnp.where(well_ids == well_row + 4, 1.0, 0.0).astype(BF16)

    loads["sat"].wait()
    loads["p"].wait()

    @pl.loop(0, NZ)
    def _(z):
        sw, sg = sat_ref[0, z], sat_ref[1, z]
        so = 1.0 - sw - sg
        total = so * so * 0.5 + sw * sw + sg * sg * 5.0
        rows = pl.ds(pl.multiple_of(z * CX, CX), CX)
        for n, part in enumerate(split(total) + split(p_ref[z])):
            fields[rows, n * CY:(n + 1) * CY] = part

    sub256 = lax.broadcasted_iota(jnp.int32, (CY, 256), 0)

    def lane_rows(ref_row, chunk):
        if ref_row == 0:
            ids = pc_ref[0:1, chunk] & 127
        else:
            w = jnp.maximum(pw_ref[0:1, chunk], 0)
            ids = ((w >> 8) & 3) * 32 + (w & 31)
        return ids

    def picked(operand, rows_ref, which, count, dst):
        for j in range(SLOTS // 256):
            chunk = slice(j * 256, (j + 1) * 256)
            g = lax.dot_general(operand, rows_ref[0:operand.shape[0], chunk], CONTRACT_FIRST, preferred_element_type=F32)
            mask = sub256 == lane_rows(which, chunk)
            for n in range(count):
                both = g[2 * n * CY:(2 * n + 1) * CY] + g[(2 * n + 1) * CY:(2 * n + 2) * CY]
                slotv[dst + n:dst + n + 1, chunk] = jnp.sum(jnp.where(mask, both, 0.0), axis=0, keepdims=True)

    def spread_lanes(value_row, which, base):
        for j in range(SLOTS // 256):
            chunk = slice(j * 256, (j + 1) * 256)
            v = jnp.where(sub256 == lane_rows(which, chunk), slotv[value_row:value_row + 1, chunk], 0.0)
            high, low = split(v)
            spread[base:base + CY, chunk] = high
            spread[base + CY:base + 2 * CY, chunk] = low

    def scatter_cells(value_row):
        spread_lanes(value_row, 0, 0)
        both = lax.dot_general(onehot[...], spread[0:256, :], CONTRACT_LAST, preferred_element_type=F32)
        wacc[...] = both[:, 0:CY] + both[:, CY:2 * CY]

    def well_sums(value_row, with_base):
        spread_lanes(value_row, 1, 0)
        both = lax.dot_general(wrow[0:64, :], spread[0:256, :], CONTRACT_LAST, preferred_element_type=F32)
        if with_base:
            spread_lanes(1, 1, 256)
            both = both + lax.dot_general(wrow[64:128, :], spread[256:512, :], CONTRACT_LAST, preferred_element_type=F32)
        sums = both[:, 0:CY] + both[:, CY:2 * CY]
        return sums.reshape(NGY, 8, CY)

    picked(fields[...], onehot, 0, 2, 4)
    factor = slotv[0:1, :] * slotv[4:5, :]
    slotv[1:2, :] = factor
    slotv[2:3, :] = factor * slotv[5:6, :]
    table[0] = well_sums(2, True)

    pl.semaphore_wait(barrier, NGX + NGY - 2)

    def send(copies):
        for copy in copies:
            copy.start()

    def arrive(copies):
        for copy in copies:
            copy.wait_recv()

    def exchange(t):
        arrive(rs_copies(t))
        part = table[t, iy]
        for n in range(NGY - 1):
            part = part + rs_recv[t, n]
        xs_src[t] = part
        send(xs_copies(t))

    def finish_sums(t):
        arrive(xs_copies(t))
        total = xs_src[t]
        for n in range(NGX - 1):
            total = total + xs_recv[t, n]
        return total

    send(rs_copies(0))

    for name in ("perm", "dep", "flag", "wm", "wt"):
        loads[name].wait()

    @pl.loop(0, NZ)
    def _(z):
        p, sw, sg = p_ref[z], sat_ref[0, z], sat_ref[1, z]
        so, bo, bw = phase_state(p, sw, sg)
        so2, sw2, sg2 = so * so * 0.5, sw * sw, sg * sg * 5.0
        m = (so2 * bo, sw2 * bw, sg2 * p)
        for c in range(3):
            mob[c, z] = m[c]
        flags = flag_ref[z]
        bit_x = (flags & 1).astype(F32)
        bit_y = ((flags >> 1) & 1).astype(F32)
        dep = dep_ref[z]
        xf = m + (perm_ref[0, z], dep, bit_x, p)
        yf = m + (perm_ref[1, z], dep, bit_y, p)
        for n, f in enumerate(xf):
            hx_send[0, z, n:n + 1, :] = f[0:1, :]
            hx_send[1, z, n:n + 1, :] = f[CX - 1:CX, :]
        hx_send[0, z, 7:8, :] = jnp.zeros((1, CY), F32)
        hx_send[1, z, 7:8, :] = jnp.zeros((1, CY), F32)
        packed = jnp.zeros((CX, CY), F32)
        for n, f in enumerate(yf):
            packed = jnp.where(lane == n, pltpu.roll(f, (n + 1) % CY, 1), packed)
            packed = jnp.where(lane == 8 + n, pltpu.roll(f, 8 + n, 1), packed)
        halo_y[z] = packed

    quarter = lax.broadcasted_iota(jnp.int32, (8, CY), 1) // 32
    line = lax.broadcasted_iota(jnp.int32, (8, CY), 0)
    own = (quarter == lax.rem(ix, 4)) & (line % 4 == ix // 4)
    target4 = jnp.concatenate([wt_ref[...]] * 4, axis=1)
    mode4 = jnp.concatenate([wm_ref[...].astype(F32)] * 4, axis=1)
    controls = jnp.where(line < 4, jnp.broadcast_to(target4, (8, CY)), jnp.broadcast_to(mode4, (8, CY)))
    tm_src[...] = jnp.where(own, controls, 0.0)

    send(tm_copies)
    turned = halo_y[...].reshape(ROWS, CY).T
    hy_send[1] = turned[0:8, :]
    hy_send[0] = turned[8:16, :]
    send(halo1)
    exchange(0)

    scatter_cells(1)
    for name in ("pv", "res"):
        loads[name].wait()
    arrive(halo1)
    stacked = jnp.concatenate([hy_recv[0], hy_recv[1], jnp.zeros((CY - 16, ROWS), F32)], axis=0)
    halo_y[...] = stacked.T.reshape(NZ, CX, CY)

    def face(w, m, n, k, kn, up, drop):
        trans = 2.0 * k * kn / (k + kn)
        c = jnp.zeros((CX, CY), F32)
        g = jnp.zeros((CX, CY), F32)
        for i in range(3):
            flux = w[i] * jnp.where(up, m[i], n[i])
            c = c + flux
            g = g + GAMMA[i] * flux
        c = c * trans
        return c, g * (trans * drop)

    @pl.loop(0, NZ)
    def _(z):
        p, sw, sg = p_ref[z], sat_ref[0, z], sat_ref[1, z]
        so, bo, bw = phase_state(p, sw, sg)
        w = (1.0 / bo, 1.0 / bw, 1.0 / p)
        m = (mob[0, z], mob[1, z], mob[2, z])
        dep = dep_ref[z]
        flags = flag_ref[z]
        storage = pv_ref[z] * (so * 0.2 * w[0] + sw * 0.05 * w[1] + sg * w[2])
        lift = jnp.zeros((CX, CY), F32)
        faces = jnp.zeros((CX, CY), F32)
        beside = jnp.zeros((CX, CY), F32)

        def add(n, lift, faces, beside, c, g, pn):
            coup[n, z] = c
            return lift + g, faces + c, beside + c * pn

        for side in range(2):
            halo = hx_recv[side, z]
            edge = 0 if side == 0 else CX - 1
            inside = (ix > 0) if side == 0 else (ix < NGX - 1)

            def shifted(f, n):
                return jnp.where(row == edge, jnp.broadcast_to(halo[n:n + 1, :], (CX, CY)), pltpu.roll(f, 1 if side == 0 else CX - 1, 0))
            k = perm_ref[0, z]
            kn = shifted(k, 3)
            kn = jnp.where((row == edge) & jnp.logical_not(inside), 0.0, kn)
            if side == 0:
                up = shifted((flags & 1).astype(F32), 5) < 0.5
            else:
                up = (flags & 1) == 1
            c, g = face(w, m, tuple(shifted(m[i], i) for i in range(3)), k, kn, up, dep - shifted(dep, 4))
            lift, faces, beside = add(side, lift, faces, beside, c, g, shifted(p, 6))

        pack = halo_y[z]
        for side in range(2):
            edge = 0 if side == 0 else CY - 1
            inside = (iy > 0) if side == 0 else (iy < NGY - 1)

            def shifted(f, n):
                moved = pltpu.roll(pack, (CY - n) % CY if side == 0 else CY - 1 - 8 - n, 1)
                return jnp.where(lane == edge, moved, pltpu.roll(f, 1 if side == 0 else CY - 1, 1))
            k = perm_ref[1, z]
            kn = shifted(k, 3)
            kn = jnp.where((lane == edge) & jnp.logical_not(inside), 0.0, kn)
            if side == 0:
                up = shifted(((flags >> 1) & 1).astype(F32), 5) < 0.5
            else:
                up = ((flags >> 1) & 1) == 1
            c, g = face(w, m, tuple(shifted(m[i], i) for i in range(3)), k, kn, up, dep - shifted(dep, 4))
            lift, faces, beside = add(2 + side, lift, faces, beside, c, g, shifted(p, 6))

        for side in range(2):
            zn = jnp.maximum(z - 1, 0) if side == 0 else jnp.minimum(z + 1, NZ - 1)
            inside = (z > 0) if side == 0 else (z < NZ - 1)
            k = perm_ref[2, z]
            kn = jnp.where(inside, perm_ref[2, zn], 0.0)
            if side == 0:
                up = (flag_ref[zn] >> 2) == 0
            else:
                up = (flags >> 2) == 1
            c, g = face(w, m, (mob[0, zn], mob[1, zn], mob[2, zn]), k, kn, up, dep - dep_ref[zn])
            lift, faces, beside = add(4 + side, lift, faces, beside, c, g, p_ref[zn])

        combined = w[0] * res_ref[0, z] + w[1] * res_ref[1, z] + w[2] * res_ref[2, z]
        b = storage * p - combined + lift
        rows = pl.ds(pl.multiple_of(z * CX, CX), CX)
        damp = 0.8 / (storage + faces + wacc[rows, :])
        rhs[z] = b
        inv[z] = damp
        pre[z] = 0.2 * p + damp * (b + beside)

    arrive(tm_copies)
    controls = tm_src[...]
    for n in range(NGX - 1):
        controls = controls + tm_recv[n]
    mode = pltpu.roll(controls, 4, 0)

    def bhp_of(sums, base):
        value = jnp.where(mode < 0.5, controls, (sums - controls) / base)
        return jnp.where(line < 4, value, 0.0)

    def slot_flow(t):
        arrive(bh_recvs(t))
        high, low = split(ball[t].reshape(64, CY))
        picked(jnp.concatenate([high, low], axis=1), wrow, 1, 1, 3)
        slotv[2:3, :] = slotv[1:2, :] * slotv[3:4, :]

    sums = finish_sums(0)
    base = pltpu.roll(sums, 4, 0)
    ball[0, iy] = bhp_of(sums, base)
    send(bh_sends(0))

    cells = jnp.broadcast_to(pc_ref[...].astype(F32), (CY, SLOTS)).T

    for j in range(SLOTS // CY):
        chunk = slice(j * CY, (j + 1) * CY)
        same[:, chunk] = jnp.where(cells == pc_ref[0:1, chunk].astype(F32), 1.0, 0.0).astype(BF16)

    @pl.loop(0, NZ)
    def _(z):
        rows = pl.ds(pl.multiple_of(z * CX, CX), CX)
        for n, part in enumerate(split(pre[z]) + split(inv[z])):
            fields[rows, n * CY:(n + 1) * CY] = part

    picked(fields[...], onehot, 0, 2, 4)
    slot_flow(0)
    high, low = split(slotv[2:3, :])
    flow = jnp.concatenate([jnp.broadcast_to(high, (16, SLOTS)), jnp.broadcast_to(low, (16, SLOTS))], axis=0)
    met = jnp.dot(flow, same[...], preferred_element_type=F32)
    slotv[6:7, :] = slotv[1:2, :] * (slotv[4:5, :] + slotv[5:6, :] * (met[0:1, :] + met[16:17, :]))
    table[1] = well_sums(6, False)
    send(rs_copies(1))

    scatter_cells(2)

    @pl.loop(0, NZ)
    def _(z):
        rows = pl.ds(pl.multiple_of(z * CX, CX), CX)
        c = pre[z] + inv[z] * wacc[rows, :]
        cur[z] = c
        hx2_send[0, z] = c[0:1, :]
        hx2_send[1, z] = c[CX - 1:CX, :]
        packed = jnp.where(lane == 0, pltpu.roll(c, 1, 1), 0.0)
        halo_y[z] = jnp.where(lane == 8, pltpu.roll(c, 8, 1), packed)

    turned = halo_y[...].reshape(ROWS, CY).T
    hy2_send[1] = turned[0:8, :]
    hy2_send[0] = turned[8:16, :]
    send(halo2)
    exchange(1)

    arrive(halo2)
    stacked = jnp.concatenate([hy2_recv[0], hy2_recv[1], jnp.zeros((CY - 16, ROWS), F32)], axis=0)
    halo_y[...] = stacked.T.reshape(NZ, CX, CY)

    @pl.loop(0, NZ)
    def _(z):
        c = cur[z]
        pack = halo_y[z]
        up_x = jnp.where(row == 0, jnp.broadcast_to(hx2_recv[0, z], (CX, CY)), pltpu.roll(c, 1, 0))
        down_x = jnp.where(row == CX - 1, jnp.broadcast_to(hx2_recv[1, z], (CX, CY)), pltpu.roll(c, CX - 1, 0))
        up_y = jnp.where(lane == 0, pack, pltpu.roll(c, 1, 1))
        down_y = jnp.where(lane == CY - 1, pltpu.roll(pack, CY - 9, 1), pltpu.roll(c, CY - 1, 1))
        up_z, down_z = cur[jnp.maximum(z - 1, 0)], cur[jnp.minimum(z + 1, NZ - 1)]
        total = rhs[z]
        for n, value in enumerate((up_x, down_x, up_y, down_y, up_z, down_z)):
            total = total + coup[n, z] * value
        pre[z] = 0.2 * c + inv[z] * total

    value = bhp_of(finish_sums(1), base)
    ball[1, iy] = value
    send(bh_sends(1))
    slot_flow(1)
    scatter_cells(2)

    @pl.loop(0, NZ)
    def _(z):
        rows = pl.ds(pl.multiple_of(z * CX, CX), CX)
        out_ref[z] = pre[z] + inv[z] * wacc[rows, :]

    mine = jnp.sum(jnp.where(own & (line < 4), value, 0.0), axis=0, keepdims=True)
    mine = jnp.broadcast_to(mine, (8, CY))
    mine = mine + pltpu.roll(mine, 32, 1) + pltpu.roll(mine, 64, 1) + pltpu.roll(mine, 96, 1)
    bhp_ref[...] = mine[0:1, 0:32]

    for copy in rs_copies(0) + rs_copies(1) + xs_copies(0) + xs_copies(1) + bh_sends(0) + bh_sends(1) + tm_copies:
        copy.wait_send()
    for copy in halo1 + halo2:
        copy.wait_send()


def body(pressure, saturation, permeability, pore_volume, cell_depth, residual, upstream_flags,
         perf_cell, perf_well, perf_index, well_mode, well_target):
    grid = (NZ, CX, CY)
    vmem = pl.BlockSpec(memory_space=pltpu.VMEM)
    dma = pltpu.SemaphoreType.DMA
    new_pressure, well_bhp = pl.pallas_call(
        kernel,
        out_shape=(pltpu.VMEM(grid, F32), pltpu.VMEM((1, 32), F32)),
        in_specs=[pl.BlockSpec(memory_space=pl.ANY)] * 12,
        out_specs=(vmem, vmem),
        scratch_shapes=[
            pltpu.VMEM(grid, F32),
            pltpu.VMEM((2,) + grid, F32),
            pltpu.VMEM((3,) + grid, F32),
            pltpu.VMEM(grid, F32),
            pltpu.VMEM(grid, F32),
            pltpu.VMEM((3,) + grid, F32),
            pltpu.VMEM(grid, jnp.int32),
            pltpu.VMEM((1, SLOTS), jnp.int32),
            pltpu.VMEM((1, SLOTS), jnp.int32),
            pltpu.VMEM((1, SLOTS), F32),
            pltpu.VMEM((1, 32), jnp.int32),
            pltpu.VMEM((1, 32), F32),
            pltpu.VMEM((3,) + grid, F32),
            pltpu.VMEM((ROWS, SLOTS), BF16),
            pltpu.VMEM((ROWS, 4 * CY), BF16),
            pltpu.VMEM((4 * CY, SLOTS), BF16),
            pltpu.VMEM((128, SLOTS), BF16),
            pltpu.VMEM((SLOTS, SLOTS), BF16),
            pltpu.VMEM((6,) + grid, F32),
            pltpu.VMEM(grid, F32),
            pltpu.VMEM(grid, F32),
            pltpu.VMEM(grid, F32),
            pltpu.VMEM(grid, F32),
            pltpu.VMEM((ROWS, CY), F32),
            pltpu.VMEM((8, SLOTS), F32),
            pltpu.VMEM((2, NGY, 8, CY), F32),
            pltpu.VMEM((2, NGY - 1, 8, CY), F32),
            pltpu.VMEM((2, 8, CY), F32),
            pltpu.VMEM((2, NGX - 1, 8, CY), F32),
            pltpu.VMEM((8, CY), F32),
            pltpu.VMEM((NGX - 1, 8, CY), F32),
            pltpu.VMEM((2, NGY, 8, CY), F32),
            pltpu.VMEM((2, NZ, 8, CY), F32),
            pltpu.VMEM((2, NZ, 8, CY), F32),
            pltpu.VMEM((2, 8, ROWS), F32),
            pltpu.VMEM((2, 8, ROWS), F32),
            pltpu.VMEM(grid, F32),
            pltpu.VMEM((2, NZ, 1, CY), F32),
            pltpu.VMEM((2, NZ, 1, CY), F32),
            pltpu.VMEM((2, 8, ROWS), F32),
            pltpu.VMEM((2, 8, ROWS), F32),
            dma((12,)),
            dma((2, NGY - 1)), dma((2, NGY - 1)),
            dma((2, NGX - 1)), dma((2, NGX - 1)),
            dma((NGX - 1,)), dma((NGX - 1,)),
            dma((2, NGY - 1)), dma((2, NGY - 1)),
            dma((8,)), dma((8,)),
        ],
        compiler_params=pltpu.CompilerParams(collective_id=0, has_side_effects=True),
        name="cpr_step",
    )(pressure, saturation, permeability, pore_volume, cell_depth, residual, upstream_flags,
      perf_cell, perf_well, perf_index, well_mode.reshape(1, 32), well_target.reshape(1, 32))
    return new_pressure, well_bhp.reshape(32)


def solution(mesh):
    areal, stacked, owned = P(None, "gx", "gy"), P(None, None, "gx", "gy"), P(("gx", "gy"))
    slots = P(("gx", "gy"), None)
    return jax.shard_map(
        body,
        mesh=mesh,
        in_specs=(areal, stacked, stacked, areal, areal, stacked, areal, slots, slots, slots, owned, owned),
        out_specs=(areal, owned),
        check_vma=False,
    )
```

time: 45.2 us -> 39.2 us (0.87)
  Pallas kernels: 42.2 us -> 37.3 us
  local copies, waits for them, and re-layouts: 2.13 us -> 1.19 us
    pallas_call x1, Pallas kernels: 42.2 us -> 37.3 us  [body(): pl.pallas_call(kernel, out_shape=(pltpu.VMEM(grid, F32), pltpu.VMEM((1, 3...]
    unnamed x4 -> x2, local copies, waits for them, and re-layouts: 2.13 us -> 1.19 us
where the time goes in v2:
time: 39.2 us; the launch traced here: 39.1 us
  Pallas kernels  37.3 us (95%)
  local copies, waits for them, and re-layouts  1.19 us (3%)
  between operations  0.64 us (2%)
    pallas_call x1, Pallas kernels, body(): pl.pallas_call(kernel, out_shape=(pltpu.VMEM(grid, F32), pltpu.VMEM((1, 3...  37.3 us
    unnamed x2, local copies, waits for them, and re-layouts  1.19 us

profile of v2, /device:TPU:1, one launch (start us, length us, event | category | flops | bytes accessed | tf_op | source)
XLA Modules:
  0.0 39.1 jit_solution(15225886029219552920)
XLA Ops:
  0.6 37.3 %cpr_step.1 = (f32[12,32,128]{2,1,0:T(8,128)S(1)}, f32[1,32]{1,0:T(1,128)S(1)}) custom-call(f32[12,32,128]{2,1,0:T(8,128)} %p_hbm.1, f32[2,12,32,128]{3,2,1,0:T(8,128)} %sat_hbm.1, f32[3,12,32,128]{3,2,1,0:T(8,128)} %perm_hbm.1, f32[12,32,128]{2,1,0:T(8,128)} %pv_hbm.1, f32[12,32,128]{2,1,0:T(8,128)} %dep_hbm.1, f32[3,12,32,128]{3,2,1,0:T(8,128)} %res_hbm.1, ...), custom_call_target="tpu_custom_call" | custom-call | tf_op jit(solution)/shard_map/cpr_step/pallas_call | solution.py:452
  37.9 0.7 %copy.16 = f32[12,32,128]{2,1,0:T(8,128)} copy(f32[12,32,128]{2,1,0:T(8,128)S(1)} %get-tuple-element.6) | data formatting | bytes 393216
  38.6 0.5 %copy.17 = f32[32]{0:T(128)} copy(f32[32]{0:T(128)S(1)} %bitcast.3) | data formatting | bytes 256

commit v3 on v2

--- a/solution.py
+++ b/solution.py
@@ -40,10 +40,10 @@
     p_hbm, sat_hbm, perm_hbm, pv_hbm, dep_hbm, res_hbm, flag_hbm, pc_hbm, pw_hbm, pi_hbm, wm_hbm, wt_hbm,
     out_ref, bhp_ref,
     p_ref, sat_ref, perm_ref, pv_ref, dep_ref, res_ref, flag_ref, pc_ref, pw_ref, pi_ref, wm_ref, wt_ref,
-    mob, onehot, fields, spread, wrow, same, coup, pre, inv, rhs, cur, wacc, slotv,
-    table, rs_recv, xs_src, xs_recv, tm_src, tm_recv, ball,
+    mob, onehot, fields, spread, wlane, wpart, same, coup, pre, inv, rhs, cur, wacc, slotv,
+    table0, table1, rs_recv0, rs_recv1, xs_src0, xs_src1, xs_recv0, xs_recv1, pair_src, pair_recv, tm_all, ctl, ball,
     hx_send, hx_recv, hy_send, hy_recv, halo_y, hx2_send, hx2_recv, hy2_send, hy2_recv,
-    in_sem, rs_ss, rs_rs, xs_ss, xs_rs, tm_ss, tm_rs, bh_ss, bh_rs, h_ss, h_rs,
+    in_sem, send_sem, recv_sem,
 ):
     ix, iy = lax.axis_index("gx"), lax.axis_index("gy")
     chip_y, chip_z = ix // 4, lax.rem(ix, 4)
@@ -76,36 +76,48 @@
         return pltpu.make_async_remote_copy(src_ref=src, dst_ref=dst, send_sem=ss, recv_sem=rs,
                                             device_id=dev, device_id_type=MESH)
 
-    def rs_copies(t):
-        return [remote(table.at[t, gy_of(a, b)], rs_recv.at[t, n], rs_ss.at[t, n], rs_rs.at[t, n], (ix, gy_of(a, b)))
-                for n, (a, b) in enumerate(GY_OFFSETS)]
-
-    def xs_copies(t):
-        return [remote(xs_src.at[t], xs_recv.at[t, n], xs_ss.at[t, n], xs_rs.at[t, n], (gx_of(a, b), iy))
-                for n, (a, b) in enumerate(GX_OFFSETS)]
-
-    tm_copies = [remote(tm_src, tm_recv.at[n], tm_ss.at[n], tm_rs.at[n], (gx_of(a, b), iy))
-                 for n, (a, b) in enumerate(GX_OFFSETS)]
-
-    def bh_sends(t):
-        return [remote(ball.at[t, iy], ball.at[t, iy], bh_ss.at[t, n], bh_rs.at[t, n], (ix, gy_of(a, b)))
-                for n, (a, b) in enumerate(GY_OFFSETS)]
-
-    def bh_recvs(t):
-        return [remote(ball.at[t, gy_of((4 - a) % 4, b)], ball.at[t, gy_of((4 - a) % 4, b)], bh_ss.at[t, n], bh_rs.at[t, n],
-                       (ix, gy_of(a, b)))
-                for n, (a, b) in enumerate(GY_OFFSETS)]
-
-    def halo_copies(xs, xr, ys, yr, base):
-        return (
-            remote(xs.at[1], xr.at[0], h_ss.at[base], h_rs.at[base], (lax.rem(ix + 1, NGX), iy)),
-            remote(xs.at[0], xr.at[1], h_ss.at[base + 1], h_rs.at[base + 1], (lax.rem(ix + NGX - 1, NGX), iy)),
-            remote(ys.at[1], yr.at[0], h_ss.at[base + 2], h_rs.at[base + 2], (ix, lax.rem(iy + 1, NGY))),
-            remote(ys.at[0], yr.at[1], h_ss.at[base + 3], h_rs.at[base + 3], (ix, lax.rem(iy + NGY - 1, NGY))),
-        )
-
-    halo1 = halo_copies(hx_send, hx_recv, hy_send, hy_recv, 0)
-    halo2 = halo_copies(hx2_send, hx2_recv, hy2_send, hy2_recv, 4)
+    table, rs_recv = (table0, table1), (rs_recv0, rs_recv1)
+    xs_src, xs_recv = (xs_src0, xs_src1), (xs_recv0, xs_recv1)
+
+    def chunk_of(a, b):
+        return lax.rem(core + b, 2) * 2 + lax.rem(chip_x + a, 2)
+
+    mine_chunk = chunk_of(0, 0)
+    far = (ix, gy_of(2, 0))
+    near = [(ix, gy_of(0, 1))] + [(ix, (chip_x + 1 - 2 * lax.rem(chip_x, 2)) * 2 + lax.rem(core + b, 2)) for b in (0, 1)]
+
+    class Group:
+        def __init__(self, sem, copies, whole):
+            self.copies = [remote(src, dst, send_sem.at[sem], recv_sem.at[sem], dev) for src, dst, dev in copies]
+            self.all = remote(whole, whole, send_sem.at[sem], recv_sem.at[sem], copies[0][2])
+
+        def send(self):
+            for copy in self.copies:
+                copy.start()
+
+        def arrive(self):
+            self.all.wait_recv()
+
+        def left(self):
+            self.all.wait_send()
+
+    rs = [Group(t, [(table[t].at[chunk_of(a, b)], rs_recv[t].at[n], (ix, gy_of(a, b))) for n, (a, b) in enumerate(GY_OFFSETS)],
+                rs_recv[t]) for t in range(2)]
+    xs = [Group(2 + t, [(xs_src[t], xs_recv[t].at[n], (gx_of(a, b), iy)) for n, (a, b) in enumerate(GX_OFFSETS)],
+                xs_recv[t]) for t in range(2)]
+    bh = [Group(4 + t, [(ball.at[t, mine_chunk], ball.at[t, mine_chunk], dev) for dev in near[::-1]], ball.at[t, 0:3])
+          for t in range(2)]
+    pair = Group(6, [(pair_src, pair_recv, far)], pair_recv)
+    tm = Group(7, [(tm_all.at[ix], tm_all.at[ix], (gx_of(a, b), iy)) for a, b in GX_OFFSETS], tm_all.at[0:NGX - 1])
+
+    def halo_group(sem, xs, xr, ys, yr):
+        after, before = (lax.rem(ix + 1, NGX), iy), (lax.rem(ix + NGX - 1, NGX), iy)
+        right, left = (ix, lax.rem(iy + 1, NGY)), (ix, lax.rem(iy + NGY - 1, NGY))
+        return (Group(sem, [(xs.at[1], xr.at[0], after), (xs.at[0], xr.at[1], before)], xr),
+                Group(sem + 1, [(ys.at[1], yr.at[0], right), (ys.at[0], yr.at[1], left)], yr))
+
+    halo1 = halo_group(8, hx_send, hx_recv, hy_send, hy_recv)
+    halo2 = halo_group(10, hx2_send, hx2_recv, hy2_send, hy2_recv)
 
     for name in ("pc", "pw", "pi"):
         loads[name].wait()
@@ -113,7 +125,10 @@
     cell_row = cell >> 7
     live = pw_ref[...] >= 0
     well = jnp.where(live, pw_ref[...], 0)
-    well_row = ((well >> 5) & 7) * 8 + (well >> 10)
+    owner = well >> 5
+    well_row = (owner & 1) * 16 + ((owner >> 1) & 1) * 8 + ((owner >> 2) & 1) * 4 + (owner >> 5)
+    well_lane = ((owner >> 3) & 3) * 32 + (well & 31)
+    well_rows = lax.broadcasted_iota(jnp.int32, (32, SLOTS), 0) == well_row
     slotv[0:1, :] = jnp.where(live, pi_ref[...], 0.0)
 
     @pl.loop(0, NZ)
@@ -121,9 +136,7 @@
         ids = lax.broadcasted_iota(jnp.int32, (CX, SLOTS), 0) + z * CX
         onehot[pl.ds(pl.multiple_of(z * CX, CX), CX), :] = jnp.where(ids == cell_row, 1.0, 0.0).astype(BF16)
 
-    well_ids = lax.broadcasted_iota(jnp.int32, (64, SLOTS), 0)
-    wrow[0:64, :] = jnp.where(well_ids == well_row, 1.0, 0.0).astype(BF16)
-    wrow[64:128, :] = jnp.where(well_ids == well_row + 4, 1.0, 0.0).astype(BF16)
+    wlane[...] = jnp.where(lax.broadcasted_iota(jnp.int32, (CY, SLOTS), 0) == well_lane, 1.0, 0.0).astype(BF16)
 
     loads["sat"].wait()
     loads["p"].wait()
@@ -139,79 +152,71 @@
 
     sub256 = lax.broadcasted_iota(jnp.int32, (CY, 256), 0)
 
-    def lane_rows(ref_row, chunk):
-        if ref_row == 0:
-            ids = pc_ref[0:1, chunk] & 127
-        else:
-            w = jnp.maximum(pw_ref[0:1, chunk], 0)
-            ids = ((w >> 8) & 3) * 32 + (w & 31)
-        return ids
-
-    def picked(operand, rows_ref, which, count, dst):
+    def picked(count, dst):
         for j in range(SLOTS // 256):
             chunk = slice(j * 256, (j + 1) * 256)
-            g = lax.dot_general(operand, rows_ref[0:operand.shape[0], chunk], CONTRACT_FIRST, preferred_element_type=F32)
-            mask = sub256 == lane_rows(which, chunk)
+            g = lax.dot_general(fields[...], onehot[:, chunk], CONTRACT_FIRST, preferred_element_type=F32)
+            mask = sub256 == (pc_ref[0:1, chunk] & 127)
             for n in range(count):
                 both = g[2 * n * CY:(2 * n + 1) * CY] + g[(2 * n + 1) * CY:(2 * n + 2) * CY]
                 slotv[dst + n:dst + n + 1, chunk] = jnp.sum(jnp.where(mask, both, 0.0), axis=0, keepdims=True)
 
-    def spread_lanes(value_row, which, base):
+    def scatter_cells(value_row):
         for j in range(SLOTS // 256):
             chunk = slice(j * 256, (j + 1) * 256)
-            v = jnp.where(sub256 == lane_rows(which, chunk), slotv[value_row:value_row + 1, chunk], 0.0)
-            high, low = split(v)
-            spread[base:base + CY, chunk] = high
-            spread[base + CY:base + 2 * CY, chunk] = low
-
-    def scatter_cells(value_row):
-        spread_lanes(value_row, 0, 0)
-        both = lax.dot_general(onehot[...], spread[0:256, :], CONTRACT_LAST, preferred_element_type=F32)
+            mask = sub256 == (pc_ref[0:1, chunk] & 127)
+            v = slotv[value_row:value_row + 1, chunk]
+            high = v.astype(BF16).astype(F32)
+            spread[0:CY, chunk] = jnp.where(mask, high, 0.0).astype(BF16)
+            spread[CY:2 * CY, chunk] = jnp.where(mask, v - high, 0.0).astype(BF16)
+        both = lax.dot_general(onehot[...], spread[...], CONTRACT_LAST, preferred_element_type=F32)
         wacc[...] = both[:, 0:CY] + both[:, CY:2 * CY]
 
-    def well_sums(value_row, with_base):
-        spread_lanes(value_row, 1, 0)
-        both = lax.dot_general(wrow[0:64, :], spread[0:256, :], CONTRACT_LAST, preferred_element_type=F32)
-        if with_base:
-            spread_lanes(1, 1, 256)
-            both = both + lax.dot_general(wrow[64:128, :], spread[256:512, :], CONTRACT_LAST, preferred_element_type=F32)
-        sums = both[:, 0:CY] + both[:, CY:2 * CY]
-        return sums.reshape(NGY, 8, CY)
-
-    picked(fields[...], onehot, 0, 2, 4)
+    def well_sums(value_rows):
+        for n, value_row in enumerate(value_rows):
+            v = slotv[value_row:value_row + 1, :]
+            high = v.astype(BF16).astype(F32)
+            wpart[64 * n:64 * n + 32, :] = jnp.where(well_rows, high, 0.0).astype(BF16)
+            wpart[64 * n + 32:64 * n + 64, :] = jnp.where(well_rows, v - high, 0.0).astype(BF16)
+        both = lax.dot_general(wpart[0:64 * len(value_rows), :], wlane[...], CONTRACT_LAST, preferred_element_type=F32)
+        return [(both[64 * n:64 * n + 32] + both[64 * n + 32:64 * n + 64]).reshape(4, 8, CY) for n in range(len(value_rows))]
+
+    picked(2, 4)
     factor = slotv[0:1, :] * slotv[4:5, :]
     slotv[1:2, :] = factor
     slotv[2:3, :] = factor * slotv[5:6, :]
-    table[0] = well_sums(2, True)
+    for n, sums in enumerate(well_sums((2, 1))):
+        table0[:, 8 * n:8 * n + 8, :] = sums
 
     pl.semaphore_wait(barrier, NGX + NGY - 2)
 
-    def send(copies):
-        for copy in copies:
-            copy.start()
-
-    def arrive(copies):
-        for copy in copies:
-            copy.wait_recv()
-
     def exchange(t):
-        arrive(rs_copies(t))
-        part = table[t, iy]
+        rs[t].arrive()
+        part = table[t][mine_chunk]
         for n in range(NGY - 1):
-            part = part + rs_recv[t, n]
-        xs_src[t] = part
-        send(xs_copies(t))
+            part = part + rs_recv[t][n]
+        xs_src[t][...] = part
+        xs[t].send()
 
     def finish_sums(t):
-        arrive(xs_copies(t))
-        total = xs_src[t]
+        xs[t].arrive()
+        total = xs_src[t][...]
         for n in range(NGX - 1):
-            total = total + xs_recv[t, n]
+            total = total + xs_recv[t][n]
         return total
 
-    send(rs_copies(0))
-
-    for name in ("perm", "dep", "flag", "wm", "wt"):
+    rs[0].send()
+
+    loads["wm"].wait()
+    loads["wt"].wait()
+    lanes = lax.broadcasted_iota(jnp.int32, (1, CY), 1)
+    target4 = jnp.concatenate([wt_ref[...]] * 4, axis=1)
+    mode4 = jnp.concatenate([wm_ref[...].astype(F32)] * 4, axis=1)
+    both = jnp.where((lanes // 32) % 2 == 0, target4, mode4)
+    pair_src[...] = jnp.where(lanes // 64 == chip_x // 2, both, 0.0)
+    pair.send()
+
+    for name in ("perm", "dep", "flag"):
         loads[name].wait()
 
     @pl.loop(0, NZ)
@@ -239,25 +244,26 @@
             packed = jnp.where(lane == 8 + n, pltpu.roll(f, 8 + n, 1), packed)
         halo_y[z] = packed
 
-    quarter = lax.broadcasted_iota(jnp.int32, (8, CY), 1) // 32
-    line = lax.broadcasted_iota(jnp.int32, (8, CY), 0)
-    own = (quarter == lax.rem(ix, 4)) & (line % 4 == ix // 4)
-    target4 = jnp.concatenate([wt_ref[...]] * 4, axis=1)
-    mode4 = jnp.concatenate([wm_ref[...].astype(F32)] * 4, axis=1)
-    controls = jnp.where(line < 4, jnp.broadcast_to(target4, (8, CY)), jnp.broadcast_to(mode4, (8, CY)))
-    tm_src[...] = jnp.where(own, controls, 0.0)
-
-    send(tm_copies)
     turned = halo_y[...].reshape(ROWS, CY).T
     hy_send[1] = turned[0:8, :]
     hy_send[0] = turned[8:16, :]
-    send(halo1)
+    for group in halo1:
+        group.send()
     exchange(0)
+    pair.arrive()
+    tm_all[ix] = pair_src[...] + pair_recv[...]
+    tm.send()
 
     scatter_cells(1)
+    cells = jnp.broadcast_to(pc_ref[...].astype(F32), (CY, SLOTS)).T
+    for j in range(SLOTS // CY):
+        chunk = slice(j * CY, (j + 1) * CY)
+        same[:, chunk] = jnp.where(cells == pc_ref[0:1, chunk].astype(F32), 1.0, 0.0).astype(BF16)
+
     for name in ("pv", "res"):
         loads[name].wait()
-    arrive(halo1)
+    for group in halo1:
+        group.arrive()
     stacked = jnp.concatenate([hy_recv[0], hy_recv[1], jnp.zeros((CY - 16, ROWS), F32)], axis=0)
     halo_y[...] = stacked.T.reshape(NZ, CX, CY)
 
@@ -342,49 +348,50 @@
         damp = 0.8 / (storage + faces + wacc[rows, :])
         rhs[z] = b
         inv[z] = damp
-        pre[z] = 0.2 * p + damp * (b + beside)
-
-    arrive(tm_copies)
-    controls = tm_src[...]
-    for n in range(NGX - 1):
-        controls = controls + tm_recv[n]
-    mode = pltpu.roll(controls, 4, 0)
+        first = 0.2 * p + damp * (b + beside)
+        pre[z] = first
+        for n, part in enumerate(split(first) + split(damp)):
+            fields[rows, n * CY:(n + 1) * CY] = part
+
+    picked(2, 4)
+
+    tm.arrive()
+    for n in range(NGX):
+        ctl[n:n + 1, :] = tm_all[n]
+    quarter = lax.broadcasted_iota(jnp.int32, (4, CY), 1) // 32
+    quads = [ctl[pl.ds(n, 4, stride=4), :] for n in range(4)]
+
+    def placed(start):
+        rows = jnp.zeros((4, CY), F32)
+        for n in range(4):
+            rows = jnp.where(quarter == n, pltpu.roll(quads[n], (32 * n - start) % CY, 1), rows)
+        return rows
+
+    target = jnp.concatenate([placed(0), placed(64)], axis=0)
+    mode = jnp.concatenate([placed(32), placed(96)], axis=0)
 
     def bhp_of(sums, base):
-        value = jnp.where(mode < 0.5, controls, (sums - controls) / base)
-        return jnp.where(line < 4, value, 0.0)
+        return jnp.where(mode < 0.5, target, (sums - target) / base)
 
     def slot_flow(t):
-        arrive(bh_recvs(t))
-        high, low = split(ball[t].reshape(64, CY))
-        picked(jnp.concatenate([high, low], axis=1), wrow, 1, 1, 3)
-        slotv[2:3, :] = slotv[1:2, :] * slotv[3:4, :]
+        bh[t].arrive()
+        wells = ball[t].reshape(32, CY)
+        high, low = split(wells)
+        g = jnp.dot(jnp.concatenate([high, low], axis=0), wlane[...], preferred_element_type=F32)
+        slot_bhp = jnp.sum(jnp.where(well_rows, g[0:32] + g[32:64], 0.0), axis=0, keepdims=True)
+        slotv[2:3, :] = slotv[1:2, :] * slot_bhp
 
     sums = finish_sums(0)
-    base = pltpu.roll(sums, 4, 0)
-    ball[0, iy] = bhp_of(sums, base)
-    send(bh_sends(0))
-
-    cells = jnp.broadcast_to(pc_ref[...].astype(F32), (CY, SLOTS)).T
-
-    for j in range(SLOTS // CY):
-        chunk = slice(j * CY, (j + 1) * CY)
-        same[:, chunk] = jnp.where(cells == pc_ref[0:1, chunk].astype(F32), 1.0, 0.0).astype(BF16)
-
-    @pl.loop(0, NZ)
-    def _(z):
-        rows = pl.ds(pl.multiple_of(z * CX, CX), CX)
-        for n, part in enumerate(split(pre[z]) + split(inv[z])):
-            fields[rows, n * CY:(n + 1) * CY] = part
-
-    picked(fields[...], onehot, 0, 2, 4)
+    base = sums[8:16]
+    ball[0, mine_chunk] = bhp_of(sums[0:8], base)
+    bh[0].send()
     slot_flow(0)
     high, low = split(slotv[2:3, :])
     flow = jnp.concatenate([jnp.broadcast_to(high, (16, SLOTS)), jnp.broadcast_to(low, (16, SLOTS))], axis=0)
     met = jnp.dot(flow, same[...], preferred_element_type=F32)
     slotv[6:7, :] = slotv[1:2, :] * (slotv[4:5, :] + slotv[5:6, :] * (met[0:1, :] + met[16:17, :]))
-    table[1] = well_sums(6, False)
-    send(rs_copies(1))
+    table1[...] = well_sums((6,))[0]
+    rs[1].send()
 
     scatter_cells(2)
 
@@ -401,10 +408,12 @@
     turned = halo_y[...].reshape(ROWS, CY).T
     hy2_send[1] = turned[0:8, :]
     hy2_send[0] = turned[8:16, :]
-    send(halo2)
+    for group in halo2:
+        group.send()
     exchange(1)
 
-    arrive(halo2)
+    for group in halo2:
+        group.arrive()
     stacked = jnp.concatenate([hy2_recv[0], hy2_recv[1], jnp.zeros((CY - 16, ROWS), F32)], axis=0)
     halo_y[...] = stacked.T.reshape(NZ, CX, CY)
 
@@ -422,9 +431,8 @@
             total = total + coup[n, z] * value
         pre[z] = 0.2 * c + inv[z] * total
 
-    value = bhp_of(finish_sums(1), base)
-    ball[1, iy] = value
-    send(bh_sends(1))
+    ball[1, mine_chunk] = bhp_of(finish_sums(1), base)
+    bh[1].send()
     slot_flow(1)
     scatter_cells(2)
 
@@ -433,15 +441,15 @@
         rows = pl.ds(pl.multiple_of(z * CX, CX), CX)
         out_ref[z] = pre[z] + inv[z] * wacc[rows, :]
 
-    mine = jnp.sum(jnp.where(own & (line < 4), value, 0.0), axis=0, keepdims=True)
-    mine = jnp.broadcast_to(mine, (8, CY))
+    line = lax.broadcasted_iota(jnp.int32, (8, CY), 0)
+    wide = lax.broadcasted_iota(jnp.int32, (8, CY), 1)
+    own = (line == (chip_x // 2) * 4 + chip_y) & (wide // 32 == chip_z)
+    mine = jnp.broadcast_to(jnp.sum(jnp.where(own, ball[1, mine_chunk], 0.0), axis=0, keepdims=True), (8, CY))
     mine = mine + pltpu.roll(mine, 32, 1) + pltpu.roll(mine, 64, 1) + pltpu.roll(mine, 96, 1)
     bhp_ref[...] = mine[0:1, 0:32]
 
-    for copy in rs_copies(0) + rs_copies(1) + xs_copies(0) + xs_copies(1) + bh_sends(0) + bh_sends(1) + tm_copies:
-        copy.wait_send()
-    for copy in halo1 + halo2:
-        copy.wait_send()
+    for group in rs + xs + bh + [pair, tm] + list(halo1 + halo2):
+        group.left()
 
 
 def body(pressure, saturation, permeability, pore_volume, cell_depth, residual, upstream_flags,
@@ -470,7 +478,8 @@
             pltpu.VMEM((3,) + grid, F32),
             pltpu.VMEM((ROWS, SLOTS), BF16),
             pltpu.VMEM((ROWS, 4 * CY), BF16),
-            pltpu.VMEM((4 * CY, SLOTS), BF16),
+            pltpu.VMEM((2 * CY, SLOTS), BF16),
+            pltpu.VMEM((CY, SLOTS), BF16),
             pltpu.VMEM((128, SLOTS), BF16),
             pltpu.VMEM((SLOTS, SLOTS), BF16),
             pltpu.VMEM((6,) + grid, F32),
@@ -480,13 +489,19 @@
             pltpu.VMEM(grid, F32),
             pltpu.VMEM((ROWS, CY), F32),
             pltpu.VMEM((8, SLOTS), F32),
-            pltpu.VMEM((2, NGY, 8, CY), F32),
-            pltpu.VMEM((2, NGY - 1, 8, CY), F32),
-            pltpu.VMEM((2, 8, CY), F32),
-            pltpu.VMEM((2, NGX - 1, 8, CY), F32),
+            pltpu.VMEM((4, 16, CY), F32),
+            pltpu.VMEM((4, 8, CY), F32),
+            pltpu.VMEM((NGY - 1, 16, CY), F32),
+            pltpu.VMEM((NGY - 1, 8, CY), F32),
+            pltpu.VMEM((16, CY), F32),
             pltpu.VMEM((8, CY), F32),
+            pltpu.VMEM((NGX - 1, 16, CY), F32),
             pltpu.VMEM((NGX - 1, 8, CY), F32),
-            pltpu.VMEM((2, NGY, 8, CY), F32),
+            pltpu.VMEM((1, CY), F32),
+            pltpu.VMEM((1, CY), F32),
+            pltpu.VMEM((NGX, 1, CY), F32),
+            pltpu.VMEM((NGX, CY), F32),
+            pltpu.VMEM((2, 4, 8, CY), F32),
             pltpu.VMEM((2, NZ, 8, CY), F32),
             pltpu.VMEM((2, NZ, 8, CY), F32),
             pltpu.VMEM((2, 8, ROWS), F32),
@@ -497,11 +512,8 @@
             pltpu.VMEM((2, 8, ROWS), F32),
             pltpu.VMEM((2, 8, ROWS), F32),
             dma((12,)),
-            dma((2, NGY - 1)), dma((2, NGY - 1)),
-            dma((2, NGX - 1)), dma((2, NGX - 1)),
-            dma((NGX - 1,)), dma((NGX - 1,)),
-            dma((2, NGY - 1)), dma((2, NGY - 1)),
-            dma((8,)), dma((8,)),
+            dma((12,)),
+            dma((12,)),
         ],
         compiler_params=pltpu.CompilerParams(collective_id=0, has_side_effects=True),
         name="cpr_step",

time: 39.2 us -> 35.9 us (0.916)
  Pallas kernels: 37.3 us -> 33.9 us
    pallas_call x1, Pallas kernels: 37.3 us -> 33.9 us  [body(): pl.pallas_call(kernel, out_shape=(pltpu.VMEM(grid, F32), pltpu.VMEM((1, 3...]
where the time goes in v3:
time: 35.9 us; the launch traced here: 35.8 us
  Pallas kernels  33.9 us (94%)
  local copies, waits for them, and re-layouts  1.19 us (3%)
  between operations  0.64 us (2%)
    pallas_call x1, Pallas kernels, body(): pl.pallas_call(kernel, out_shape=(pltpu.VMEM(grid, F32), pltpu.VMEM((1, 3...  33.9 us
    unnamed x2, local copies, waits for them, and re-layouts  1.19 us

profile of v3, /device:TPU:1, one launch (start us, length us, event | category | flops | bytes accessed | tf_op | source)
XLA Modules:
  0.0 35.8 jit_solution(2013933266130320833)
XLA Ops:
  0.6 33.9 %cpr_step.1 = (f32[12,32,128]{2,1,0:T(8,128)S(1)}, f32[1,32]{1,0:T(1,128)S(1)}) custom-call(f32[12,32,128]{2,1,0:T(8,128)} %p_hbm.1, f32[2,12,32,128]{3,2,1,0:T(8,128)} %sat_hbm.1, f32[3,12,32,128]{3,2,1,0:T(8,128)} %perm_hbm.1, f32[12,32,128]{2,1,0:T(8,128)} %pv_hbm.1, f32[12,32,128]{2,1,0:T(8,128)} %dep_hbm.1, f32[3,12,32,128]{3,2,1,0:T(8,128)} %res_hbm.1, ...), custom_call_target="tpu_custom_call" | custom-call | tf_op jit(solution)/shard_map/cpr_step/pallas_call | solution.py:460
  34.6 0.7 %copy.16 = f32[12,32,128]{2,1,0:T(8,128)} copy(f32[12,32,128]{2,1,0:T(8,128)S(1)} %get-tuple-element.6) | data formatting | bytes 393216
  35.3 0.5 %copy.17 = f32[32]{0:T(128)} copy(f32[32]{0:T(128)S(1)} %bitcast.3) | data formatting | bytes 256

commit v4 on v3

--- a/solution.py
+++ b/solution.py
@@ -40,7 +40,7 @@
     p_hbm, sat_hbm, perm_hbm, pv_hbm, dep_hbm, res_hbm, flag_hbm, pc_hbm, pw_hbm, pi_hbm, wm_hbm, wt_hbm,
     out_ref, bhp_ref,
     p_ref, sat_ref, perm_ref, pv_ref, dep_ref, res_ref, flag_ref, pc_ref, pw_ref, pi_ref, wm_ref, wt_ref,
-    mob, onehot, fields, spread, wlane, wpart, same, coup, pre, inv, rhs, cur, wacc, slotv,
+    mob, onehot, fields, wlane, wpart, same, coup, pre, inv, rhs, cur, wacc, slotv,
     table0, table1, rs_recv0, rs_recv1, xs_src0, xs_src1, xs_recv0, xs_recv1, pair_src, pair_recv, tm_all, ctl, ball,
     hx_send, hx_recv, hy_send, hy_recv, halo_y, hx2_send, hx2_recv, hy2_send, hy2_recv,
     in_sem, send_sem, recv_sem,
@@ -79,12 +79,8 @@
     table, rs_recv = (table0, table1), (rs_recv0, rs_recv1)
     xs_src, xs_recv = (xs_src0, xs_src1), (xs_recv0, xs_recv1)
 
-    def chunk_of(a, b):
-        return lax.rem(core + b, 2) * 2 + lax.rem(chip_x + a, 2)
-
-    mine_chunk = chunk_of(0, 0)
-    far = (ix, gy_of(2, 0))
-    near = [(ix, gy_of(0, 1))] + [(ix, (chip_x + 1 - 2 * lax.rem(chip_x, 2)) * 2 + lax.rem(core + b, 2)) for b in (0, 1)]
+    partner = (ix, gy_of(0, 1))
+    x_peers = ((2, 0), (1, 0), (3, 0))
 
     class Group:
         def __init__(self, sem, copies, whole):
@@ -101,13 +97,13 @@
         def left(self):
             self.all.wait_send()
 
-    rs = [Group(t, [(table[t].at[chunk_of(a, b)], rs_recv[t].at[n], (ix, gy_of(a, b))) for n, (a, b) in enumerate(GY_OFFSETS)],
+    rs = [Group(t, [(table[t].at[lax.rem(core + b, 2)], rs_recv[t].at[n], (ix, gy_of(a, b))) for n, (a, b) in enumerate(GY_OFFSETS)],
                 rs_recv[t]) for t in range(2)]
     xs = [Group(2 + t, [(xs_src[t], xs_recv[t].at[n], (gx_of(a, b), iy)) for n, (a, b) in enumerate(GX_OFFSETS)],
                 xs_recv[t]) for t in range(2)]
-    bh = [Group(4 + t, [(ball.at[t, mine_chunk], ball.at[t, mine_chunk], dev) for dev in near[::-1]], ball.at[t, 0:3])
+    bh = [Group(4 + t, [(ball.at[t, core], ball.at[t, core], partner)], ball.at[t, 1 - core])
           for t in range(2)]
-    pair = Group(6, [(pair_src, pair_recv, far)], pair_recv)
+    pair = Group(6, [(pair_src, pair_recv.at[n], (ix, gy_of(a, b))) for n, (a, b) in enumerate(x_peers)], pair_recv)
     tm = Group(7, [(tm_all.at[ix], tm_all.at[ix], (gx_of(a, b), iy)) for a, b in GX_OFFSETS], tm_all.at[0:NGX - 1])
 
     def halo_group(sem, xs, xr, ys, yr):
@@ -126,7 +122,7 @@
     live = pw_ref[...] >= 0
     well = jnp.where(live, pw_ref[...], 0)
     owner = well >> 5
-    well_row = (owner & 1) * 16 + ((owner >> 1) & 1) * 8 + ((owner >> 2) & 1) * 4 + (owner >> 5)
+    well_row = (owner & 1) * 16 + ((owner >> 1) & 3) * 4 + (owner >> 5)
     well_lane = ((owner >> 3) & 3) * 32 + (well & 31)
     well_rows = lax.broadcasted_iota(jnp.int32, (32, SLOTS), 0) == well_row
     slotv[0:1, :] = jnp.where(live, pi_ref[...], 0.0)
@@ -161,16 +157,17 @@
                 both = g[2 * n * CY:(2 * n + 1) * CY] + g[(2 * n + 1) * CY:(2 * n + 2) * CY]
                 slotv[dst + n:dst + n + 1, chunk] = jnp.sum(jnp.where(mask, both, 0.0), axis=0, keepdims=True)
 
-    def scatter_cells(value_row):
+    def scattered(value_row):
+        total = None
         for j in range(SLOTS // 256):
             chunk = slice(j * 256, (j + 1) * 256)
             mask = sub256 == (pc_ref[0:1, chunk] & 127)
             v = slotv[value_row:value_row + 1, chunk]
             high = v.astype(BF16).astype(F32)
-            spread[0:CY, chunk] = jnp.where(mask, high, 0.0).astype(BF16)
-            spread[CY:2 * CY, chunk] = jnp.where(mask, v - high, 0.0).astype(BF16)
-        both = lax.dot_general(onehot[...], spread[...], CONTRACT_LAST, preferred_element_type=F32)
-        wacc[...] = both[:, 0:CY] + both[:, CY:2 * CY]
+            spread = jnp.concatenate([jnp.where(mask, high, 0.0).astype(BF16), jnp.where(mask, v - high, 0.0).astype(BF16)], axis=0)
+            part = lax.dot_general(onehot[:, chunk], spread, CONTRACT_LAST, preferred_element_type=F32)
+            total = part if total is None else total + part
+        return total[:, 0:CY] + total[:, CY:2 * CY]
 
     def well_sums(value_rows):
         for n, value_row in enumerate(value_rows):
@@ -179,20 +176,34 @@
             wpart[64 * n:64 * n + 32, :] = jnp.where(well_rows, high, 0.0).astype(BF16)
             wpart[64 * n + 32:64 * n + 64, :] = jnp.where(well_rows, v - high, 0.0).astype(BF16)
         both = lax.dot_general(wpart[0:64 * len(value_rows), :], wlane[...], CONTRACT_LAST, preferred_element_type=F32)
-        return [(both[64 * n:64 * n + 32] + both[64 * n + 32:64 * n + 64]).reshape(4, 8, CY) for n in range(len(value_rows))]
+        return [(both[64 * n:64 * n + 32] + both[64 * n + 32:64 * n + 64]).reshape(2, 16, CY) for n in range(len(value_rows))]
 
     picked(2, 4)
     factor = slotv[0:1, :] * slotv[4:5, :]
     slotv[1:2, :] = factor
     slotv[2:3, :] = factor * slotv[5:6, :]
     for n, sums in enumerate(well_sums((2, 1))):
-        table0[:, 8 * n:8 * n + 8, :] = sums
+        table0[:, 16 * n:16 * n + 16, :] = sums
+
+    cells = jnp.broadcast_to(pc_ref[...].astype(F32), (CY, SLOTS)).T
+    for j in range(SLOTS // CY):
+        chunk = slice(j * CY, (j + 1) * CY)
+        same[:, chunk] = jnp.where(cells == pc_ref[0:1, chunk].astype(F32), 1.0, 0.0).astype(BF16)
+
+    loads["wm"].wait()
+    loads["wt"].wait()
+    pair_lane = lax.broadcasted_iota(jnp.int32, (2, CY), 1)
+    pair_row = lax.broadcasted_iota(jnp.int32, (2, CY), 0)
+    target4 = jnp.broadcast_to(jnp.concatenate([wt_ref[...]] * 4, axis=1), (2, CY))
+    mode4 = jnp.broadcast_to(jnp.concatenate([wm_ref[...].astype(F32)] * 4, axis=1), (2, CY))
+    both = jnp.where((pair_lane // 32) % 2 == 0, target4, mode4)
+    pair_src[...] = jnp.where((pair_row == chip_x // 2) & (pair_lane // 64 == lax.rem(chip_x, 2)), both, 0.0)
 
     pl.semaphore_wait(barrier, NGX + NGY - 2)
 
     def exchange(t):
         rs[t].arrive()
-        part = table[t][mine_chunk]
+        part = table[t][core]
         for n in range(NGY - 1):
             part = part + rs_recv[t][n]
         xs_src[t][...] = part
@@ -205,16 +216,8 @@
             total = total + xs_recv[t][n]
         return total
 
+    pair.send()
     rs[0].send()
-
-    loads["wm"].wait()
-    loads["wt"].wait()
-    lanes = lax.broadcasted_iota(jnp.int32, (1, CY), 1)
-    target4 = jnp.concatenate([wt_ref[...]] * 4, axis=1)
-    mode4 = jnp.concatenate([wm_ref[...].astype(F32)] * 4, axis=1)
-    both = jnp.where((lanes // 32) % 2 == 0, target4, mode4)
-    pair_src[...] = jnp.where(lanes // 64 == chip_x // 2, both, 0.0)
-    pair.send()
 
     for name in ("perm", "dep", "flag"):
         loads[name].wait()
@@ -249,16 +252,11 @@
     hy_send[0] = turned[8:16, :]
     for group in halo1:
         group.send()
+    wacc[...] = scattered(1)
+    pair.arrive()
+    tm_all[ix] = pair_src[...] + pair_recv[0] + pair_recv[1] + pair_recv[2]
+    tm.send()
     exchange(0)
-    pair.arrive()
-    tm_all[ix] = pair_src[...] + pair_recv[...]
-    tm.send()
-
-    scatter_cells(1)
-    cells = jnp.broadcast_to(pc_ref[...].astype(F32), (CY, SLOTS)).T
-    for j in range(SLOTS // CY):
-        chunk = slice(j * CY, (j + 1) * CY)
-        same[:, chunk] = jnp.where(cells == pc_ref[0:1, chunk].astype(F32), 1.0, 0.0).astype(BF16)
 
     for name in ("pv", "res"):
         loads[name].wait()
@@ -357,18 +355,21 @@
 
     tm.arrive()
     for n in range(NGX):
-        ctl[n:n + 1, :] = tm_all[n]
+        ctl[0, n:n + 1, :] = tm_all[n, 0:1, :]
+        ctl[1, n:n + 1, :] = tm_all[n, 1:2, :]
     quarter = lax.broadcasted_iota(jnp.int32, (4, CY), 1) // 32
-    quads = [ctl[pl.ds(n, 4, stride=4), :] for n in range(4)]
+    quads = [[ctl[h, pl.ds(n, 4, stride=4), :] for n in range(4)] for h in range(2)]
 
     def placed(start):
-        rows = jnp.zeros((4, CY), F32)
-        for n in range(4):
-            rows = jnp.where(quarter == n, pltpu.roll(quads[n], (32 * n - start) % CY, 1), rows)
-        return rows
-
-    target = jnp.concatenate([placed(0), placed(64)], axis=0)
-    mode = jnp.concatenate([placed(32), placed(96)], axis=0)
+        blocks = []
+        for x in range(4):
+            rows = jnp.zeros((4, CY), F32)
+            for n in range(4):
+                rows = jnp.where(quarter == n, pltpu.roll(quads[x // 2][n], (32 * n - start - 64 * (x % 2)) % CY, 1), rows)
+            blocks.append(rows)
+        return jnp.concatenate(blocks, axis=0)
+
+    target, mode = placed(0), placed(32)
 
     def bhp_of(sums, base):
         return jnp.where(mode < 0.5, target, (sums - target) / base)
@@ -382,8 +383,8 @@
         slotv[2:3, :] = slotv[1:2, :] * slot_bhp
 
     sums = finish_sums(0)
-    base = sums[8:16]
-    ball[0, mine_chunk] = bhp_of(sums[0:8], base)
+    base = sums[16:32]
+    ball[0, core] = bhp_of(sums[0:16], base)
     bh[0].send()
     slot_flow(0)
     high, low = split(slotv[2:3, :])
@@ -393,7 +394,7 @@
     table1[...] = well_sums((6,))[0]
     rs[1].send()
 
-    scatter_cells(2)
+    wacc[...] = scattered(2)
 
     @pl.loop(0, NZ)
     def _(z):
@@ -431,25 +432,28 @@
             total = total + coup[n, z] * value
         pre[z] = 0.2 * c + inv[z] * total
 
-    ball[1, mine_chunk] = bhp_of(finish_sums(1), base)
+    ball[1, core] = bhp_of(finish_sums(1), base)
     bh[1].send()
     slot_flow(1)
-    scatter_cells(2)
-
-    @pl.loop(0, NZ)
-    def _(z):
-        rows = pl.ds(pl.multiple_of(z * CX, CX), CX)
-        out_ref[z] = pre[z] + inv[z] * wacc[rows, :]
-
-    line = lax.broadcasted_iota(jnp.int32, (8, CY), 0)
-    wide = lax.broadcasted_iota(jnp.int32, (8, CY), 1)
-    own = (line == (chip_x // 2) * 4 + chip_y) & (wide // 32 == chip_z)
-    mine = jnp.broadcast_to(jnp.sum(jnp.where(own, ball[1, mine_chunk], 0.0), axis=0, keepdims=True), (8, CY))
+    out_ref[...] = pre[...] + inv[...] * scattered(2).reshape(NZ, CX, CY)
+
+    line = lax.broadcasted_iota(jnp.int32, (16, CY), 0)
+    wide = lax.broadcasted_iota(jnp.int32, (16, CY), 1)
+    own = (line == chip_x * 4 + chip_y) & (wide // 32 == chip_z)
+    mine = jnp.broadcast_to(jnp.sum(jnp.where(own, ball[1, core], 0.0), axis=0, keepdims=True), (8, CY))
     mine = mine + pltpu.roll(mine, 32, 1) + pltpu.roll(mine, 64, 1) + pltpu.roll(mine, 96, 1)
     bhp_ref[...] = mine[0:1, 0:32]
 
     for group in rs + xs + bh + [pair, tm] + list(halo1 + halo2):
         group.left()
+
+
+def hand_over(p_src, bhp_src, p_dst, bhp_dst, sem):
+    copies = (pltpu.make_async_copy(p_src, p_dst, sem.at[0]), pltpu.make_async_copy(bhp_src, bhp_dst, sem.at[1]))
+    for copy in copies:
+        copy.start()
+    for copy in copies:
+        copy.wait()
 
 
 def body(pressure, saturation, permeability, pore_volume, cell_depth, residual, upstream_flags,
@@ -478,7 +482,6 @@
             pltpu.VMEM((3,) + grid, F32),
             pltpu.VMEM((ROWS, SLOTS), BF16),
             pltpu.VMEM((ROWS, 4 * CY), BF16),
-            pltpu.VMEM((2 * CY, SLOTS), BF16),
             pltpu.VMEM((CY, SLOTS), BF16),
             pltpu.VMEM((128, SLOTS), BF16),
             pltpu.VMEM((SLOTS, SLOTS), BF16),
@@ -489,19 +492,19 @@
             pltpu.VMEM(grid, F32),
             pltpu.VMEM((ROWS, CY), F32),
             pltpu.VMEM((8, SLOTS), F32),
-            pltpu.VMEM((4, 16, CY), F32),
-            pltpu.VMEM((4, 8, CY), F32),
+            pltpu.VMEM((2, 32, CY), F32),
+            pltpu.VMEM((2, 16, CY), F32),
+            pltpu.VMEM((NGY - 1, 32, CY), F32),
             pltpu.VMEM((NGY - 1, 16, CY), F32),
-            pltpu.VMEM((NGY - 1, 8, CY), F32),
+            pltpu.VMEM((32, CY), F32),
             pltpu.VMEM((16, CY), F32),
-            pltpu.VMEM((8, CY), F32),
+            pltpu.VMEM((NGX - 1, 32, CY), F32),
             pltpu.VMEM((NGX - 1, 16, CY), F32),
-            pltpu.VMEM((NGX - 1, 8, CY), F32),
-            pltpu.VMEM((1, CY), F32),
-            pltpu.VMEM((1, CY), F32),
-            pltpu.VMEM((NGX, 1, CY), F32),
-            pltpu.VMEM((NGX, CY), F32),
-            pltpu.VMEM((2, 4, 8, CY), F32),
+            pltpu.VMEM((2, CY), F32),
+            pltpu.VMEM((3, 2, CY), F32),
+            pltpu.VMEM((NGX, 2, CY), F32),
+            pltpu.VMEM((2, NGX, CY), F32),
+            pltpu.VMEM((2, 2, 16, CY), F32),
             pltpu.VMEM((2, NZ, 8, CY), F32),
             pltpu.VMEM((2, NZ, 8, CY), F32),
             pltpu.VMEM((2, 8, ROWS), F32),
@@ -519,6 +522,15 @@
         name="cpr_step",
     )(pressure, saturation, permeability, pore_volume, cell_depth, residual, upstream_flags,
       perf_cell, perf_well, perf_index, well_mode.reshape(1, 32), well_target.reshape(1, 32))
+    anywhere = pl.BlockSpec(memory_space=pl.ANY)
+    new_pressure, well_bhp = pl.pallas_call(
+        hand_over,
+        out_shape=(jax.ShapeDtypeStruct(grid, F32), jax.ShapeDtypeStruct((1, 32), F32)),
+        in_specs=[vmem] * 2,
+        out_specs=(anywhere, anywhere),
+        scratch_shapes=[dma((2,))],
+        name="hand_over",
+    )(pltpu.with_memory_space_constraint(new_pressure, pltpu.VMEM), pltpu.with_memory_space_constraint(well_bhp, pltpu.VMEM))
     return new_pressure, well_bhp.reshape(32)
 
 

time: 35.9 us -> 32.5 us (0.905)
  Pallas kernels: 33.9 us -> 31.7 us
  local copies, waits for them, and re-layouts: 1.19 us -> 0 us
    pallas_call x1, Pallas kernels: 33.9 us -> 31 us  [body(): pl.pallas_call(kernel, out_shape=(pltpu.VMEM(grid, F32), pltpu.VMEM((1, 3...]
    unnamed x2 -> x0, local copies, waits for them, and re-layouts: 1.19 us -> none
    pallas_call x0 -> x1, Pallas kernels: none -> 0.7 us  [body(): pl.pallas_call(hand_over, out_shape=(jax.ShapeDtypeStruct(grid, F32), jax...]
where the time goes in v4:
time: 32.5 us; the launch traced here: 32.3 us
  Pallas kernels  31.7 us (98%)
  between operations  0.64 us (2%)
    pallas_call x1, Pallas kernels, body(): pl.pallas_call(kernel, out_shape=(pltpu.VMEM(grid, F32), pltpu.VMEM((1, 3...  31 us
    pallas_call x1, Pallas kernels, body(): pl.pallas_call(hand_over, out_shape=(jax.ShapeDtypeStruct(grid, F32), jax...  0.7 us

profile of v4, /device:TPU:1, one launch (start us, length us, event | category | flops | bytes accessed | tf_op | source)
XLA Modules:
  0.0 32.3 jit_solution(2967221784787205422)
XLA Ops:
  0.6 31.0 %cpr_step.1 = (f32[12,32,128]{2,1,0:T(8,128)S(1)}, f32[1,32]{1,0:T(1,128)S(1)}) custom-call(f32[12,32,128]{2,1,0:T(8,128)} %p_hbm.1, f32[2,12,32,128]{3,2,1,0:T(8,128)} %sat_hbm.1, f32[3,12,32,128]{3,2,1,0:T(8,128)} %perm_hbm.1, f32[12,32,128]{2,1,0:T(8,128)} %pv_hbm.1, f32[12,32,128]{2,1,0:T(8,128)} %dep_hbm.1, f32[3,12,32,128]{3,2,1,0:T(8,128)} %res_hbm.1, ...), custom_call_target="tpu_custom_call" | custom-call | tf_op jit(solution)/shard_map/cpr_step/pallas_call | solution.py:464
  31.6 0.7 %hand_over.1 = (f32[12,32,128]{2,1,0:T(8,128)}, f32[1,32]{1,0:T(1,128)}) custom-call(f32[12,32,128]{2,1,0:T(8,128)S(1)} %get-tuple-element.6.p_src, f32[1,32]{1,0:T(1,128)S(1)} %get-tuple-element.7.bhp_src), custom_call_target="tpu_custom_call" | custom-call | tf_op jit(solution)/shard_map/hand_over/pallas_call | solution.py:526

commit v5 on v4

--- a/solution.py
+++ b/solution.py
@@ -28,6 +28,11 @@
     return so, bo, bw
 
 
+def phase_mobility(p, sw, sg):
+    so, bo, bw = phase_state(p, sw, sg)
+    return so * so * 0.5 * bo, sw * sw * bw, sg * sg * 5.0 * p
+
+
 def hops(offset, size):
     return min(offset, size - offset)
 
@@ -40,9 +45,9 @@
     p_hbm, sat_hbm, perm_hbm, pv_hbm, dep_hbm, res_hbm, flag_hbm, pc_hbm, pw_hbm, pi_hbm, wm_hbm, wt_hbm,
     out_ref, bhp_ref,
     p_ref, sat_ref, perm_ref, pv_ref, dep_ref, res_ref, flag_ref, pc_ref, pw_ref, pi_ref, wm_ref, wt_ref,
-    mob, onehot, fields, wlane, wpart, same, coup, pre, inv, rhs, cur, wacc, slotv,
+    mob, onehot, fields, wlane, clane, wrow, wpart, same, coup, pre, inv, rhs, cur, wacc, slotv,
     table0, table1, rs_recv0, rs_recv1, xs_src0, xs_src1, xs_recv0, xs_recv1, pair_src, pair_recv, tm_all, ctl, ball,
-    hx_send, hx_recv, hy_send, hy_recv, halo_y, hx2_send, hx2_recv, hy2_send, hy2_recv,
+    hx_send, hx_recv, hx_mob, hy_send, hy_recv, hy_rows, halo_y, hx2_send, hx2_recv, hy2_send, hy2_recv,
     in_sem, send_sem, recv_sem,
 ):
     ix, iy = lax.axis_index("gx"), lax.axis_index("gy")
@@ -55,18 +60,23 @@
     def gy_of(a, b):
         return lax.rem(chip_x + a, 4) * 2 + lax.rem(core + b, 2)
 
+    loads = {}
+    pairs = (("pc", pc_hbm, pc_ref), ("pw", pw_hbm, pw_ref), ("pi", pi_hbm, pi_ref), ("sw", sat_hbm.at[0], sat_ref.at[0]),
+             ("sg", sat_hbm.at[1], sat_ref.at[1]), ("p", p_hbm, p_ref), ("wm", wm_hbm, wm_ref), ("wt", wt_hbm, wt_ref),
+             ("perm", perm_hbm, perm_ref), ("dep", dep_hbm, dep_ref), ("flag", flag_hbm, flag_ref),
+             ("pv", pv_hbm, pv_ref), ("res", res_hbm, res_ref))
+    for n, (name, src, dst) in enumerate(pairs):
+        loads[name] = pltpu.make_async_copy(src, dst, in_sem.at[n])
+    for name in ("pc", "pw", "pi", "sw", "sg", "p"):
+        loads[name].start()
+
     barrier = pltpu.get_barrier_semaphore()
     for a, b in GX_OFFSETS:
         pl.semaphore_signal(barrier, inc=1, device_id=(gx_of(a, b), iy), device_id_type=MESH)
     for a, b in GY_OFFSETS:
         pl.semaphore_signal(barrier, inc=1, device_id=(ix, gy_of(a, b)), device_id_type=MESH)
 
-    loads = {}
-    pairs = (("pc", pc_hbm, pc_ref), ("pw", pw_hbm, pw_ref), ("pi", pi_hbm, pi_ref), ("sat", sat_hbm, sat_ref),
-             ("p", p_hbm, p_ref), ("perm", perm_hbm, perm_ref), ("dep", dep_hbm, dep_ref), ("flag", flag_hbm, flag_ref),
-             ("wm", wm_hbm, wm_ref), ("wt", wt_hbm, wt_ref), ("pv", pv_hbm, pv_ref), ("res", res_hbm, res_ref))
-    for n, (name, src, dst) in enumerate(pairs):
-        loads[name] = pltpu.make_async_copy(src, dst, in_sem.at[n])
+    for name in ("wm", "wt", "perm", "dep", "flag", "pv", "res"):
         loads[name].start()
 
     lane = lax.broadcasted_iota(jnp.int32, (CX, CY), 1)
@@ -125,6 +135,7 @@
     well_row = (owner & 1) * 16 + ((owner >> 1) & 3) * 4 + (owner >> 5)
     well_lane = ((owner >> 3) & 3) * 32 + (well & 31)
     well_rows = lax.broadcasted_iota(jnp.int32, (32, SLOTS), 0) == well_row
+    wrow[...] = jnp.where(well_rows, 1.0, 0.0).astype(BF16)
     slotv[0:1, :] = jnp.where(live, pi_ref[...], 0.0)
 
     @pl.loop(0, NZ)
@@ -134,8 +145,10 @@
 
     wlane[...] = jnp.where(lax.broadcasted_iota(jnp.int32, (CY, SLOTS), 0) == well_lane, 1.0, 0.0).astype(BF16)
 
-    loads["sat"].wait()
-    loads["p"].wait()
+    clane[...] = jnp.where(lax.broadcasted_iota(jnp.int32, (CY, SLOTS), 0) == (cell & 127), 1.0, 0.0).astype(BF16)
+
+    for name in ("sw", "sg", "p"):
+        loads[name].wait()
 
     @pl.loop(0, NZ)
     def _(z):
@@ -161,20 +174,17 @@
         total = None
         for j in range(SLOTS // 256):
             chunk = slice(j * 256, (j + 1) * 256)
-            mask = sub256 == (pc_ref[0:1, chunk] & 127)
-            v = slotv[value_row:value_row + 1, chunk]
-            high = v.astype(BF16).astype(F32)
-            spread = jnp.concatenate([jnp.where(mask, high, 0.0).astype(BF16), jnp.where(mask, v - high, 0.0).astype(BF16)], axis=0)
+            high, low = split(slotv[value_row:value_row + 1, chunk])
+            spread = jnp.concatenate([clane[:, chunk] * high, clane[:, chunk] * low], axis=0)
             part = lax.dot_general(onehot[:, chunk], spread, CONTRACT_LAST, preferred_element_type=F32)
             total = part if total is None else total + part
         return total[:, 0:CY] + total[:, CY:2 * CY]
 
     def well_sums(value_rows):
         for n, value_row in enumerate(value_rows):
-            v = slotv[value_row:value_row + 1, :]
-            high = v.astype(BF16).astype(F32)
-            wpart[64 * n:64 * n + 32, :] = jnp.where(well_rows, high, 0.0).astype(BF16)
-            wpart[64 * n + 32:64 * n + 64, :] = jnp.where(well_rows, v - high, 0.0).astype(BF16)
+            high, low = split(slotv[value_row:value_row + 1, :])
+            wpart[64 * n:64 * n + 32, :] = wrow[...] * high
+            wpart[64 * n + 32:64 * n + 64, :] = wrow[...] * low
         both = lax.dot_general(wpart[0:64 * len(value_rows), :], wlane[...], CONTRACT_LAST, preferred_element_type=F32)
         return [(both[64 * n:64 * n + 32] + both[64 * n + 32:64 * n + 64]).reshape(2, 16, CY) for n in range(len(value_rows))]
 
@@ -184,11 +194,6 @@
     slotv[2:3, :] = factor * slotv[5:6, :]
     for n, sums in enumerate(well_sums((2, 1))):
         table0[:, 16 * n:16 * n + 16, :] = sums
-
-    cells = jnp.broadcast_to(pc_ref[...].astype(F32), (CY, SLOTS)).T
-    for j in range(SLOTS // CY):
-        chunk = slice(j * CY, (j + 1) * CY)
-        same[:, chunk] = jnp.where(cells == pc_ref[0:1, chunk].astype(F32), 1.0, 0.0).astype(BF16)
 
     loads["wm"].wait()
     loads["wt"].wait()
@@ -221,28 +226,20 @@
 
     for name in ("perm", "dep", "flag"):
         loads[name].wait()
-
-    @pl.loop(0, NZ)
-    def _(z):
-        p, sw, sg = p_ref[z], sat_ref[0, z], sat_ref[1, z]
-        so, bo, bw = phase_state(p, sw, sg)
-        so2, sw2, sg2 = so * so * 0.5, sw * sw, sg * sg * 5.0
-        m = (so2 * bo, sw2 * bw, sg2 * p)
-        for c in range(3):
-            mob[c, z] = m[c]
-        flags = flag_ref[z]
-        bit_x = (flags & 1).astype(F32)
-        bit_y = ((flags >> 1) & 1).astype(F32)
-        dep = dep_ref[z]
-        xf = m + (perm_ref[0, z], dep, bit_x, p)
-        yf = m + (perm_ref[1, z], dep, bit_y, p)
-        for n, f in enumerate(xf):
-            hx_send[0, z, n:n + 1, :] = f[0:1, :]
-            hx_send[1, z, n:n + 1, :] = f[CX - 1:CX, :]
-        hx_send[0, z, 7:8, :] = jnp.zeros((1, CY), F32)
-        hx_send[1, z, 7:8, :] = jnp.zeros((1, CY), F32)
+    for z in range(NZ):
+        for side, edge in enumerate((0, CX - 1)):
+            at = slice(edge, edge + 1)
+            rim = (p_ref[z, at, :], sat_ref[0, z, at, :], sat_ref[1, z, at, :], perm_ref[0, z, at, :], dep_ref[z, at, :],
+                   (flag_ref[z, at, :] & 1).astype(F32))
+            for n, f in enumerate(rim):
+                hx_send[side, n, z:z + 1, :] = f
+    halo1[0].send()
+
+    @pl.loop(0, NZ)
+    def _(z):
+        rim = (p_ref[z], sat_ref[0, z], sat_ref[1, z], perm_ref[1, z], dep_ref[z], ((flag_ref[z] >> 1) & 1).astype(F32))
         packed = jnp.zeros((CX, CY), F32)
-        for n, f in enumerate(yf):
+        for n, f in enumerate(rim):
             packed = jnp.where(lane == n, pltpu.roll(f, (n + 1) % CY, 1), packed)
             packed = jnp.where(lane == 8 + n, pltpu.roll(f, 8 + n, 1), packed)
         halo_y[z] = packed
@@ -250,8 +247,19 @@
     turned = halo_y[...].reshape(ROWS, CY).T
     hy_send[1] = turned[0:8, :]
     hy_send[0] = turned[8:16, :]
-    for group in halo1:
-        group.send()
+    halo1[1].send()
+
+    @pl.loop(0, NZ)
+    def _(z):
+        p, sw, sg = p_ref[z], sat_ref[0, z], sat_ref[1, z]
+        for c, m in enumerate(phase_mobility(p, sw, sg)):
+            mob[c, z] = m
+
+    cells = jnp.broadcast_to(pc_ref[...].astype(F32), (CY, SLOTS)).T
+    for j in range(SLOTS // CY):
+        chunk = slice(j * CY, (j + 1) * CY)
+        same[:, chunk] = jnp.where(cells == pc_ref[0:1, chunk].astype(F32), 1.0, 0.0).astype(BF16)
+
     wacc[...] = scattered(1)
     pair.arrive()
     tm_all[ix] = pair_src[...] + pair_recv[0] + pair_recv[1] + pair_recv[2]
@@ -262,7 +270,14 @@
         loads[name].wait()
     for group in halo1:
         group.arrive()
-    stacked = jnp.concatenate([hy_recv[0], hy_recv[1], jnp.zeros((CY - 16, ROWS), F32)], axis=0)
+    for side in range(2):
+        for c, m in enumerate(phase_mobility(hx_recv[side, 0], hx_recv[side, 1], hx_recv[side, 2])):
+            hx_mob[side, c] = m
+        got = hy_recv[side]
+        beside = phase_mobility(got[0:1], got[1:2], got[2:3]) + (got[3:4], got[4:5], got[5:6], got[0:1], got[7:8])
+        for n, f in enumerate(beside):
+            hy_rows[8 * side + n:8 * side + n + 1, :] = f
+    stacked = jnp.concatenate([hy_rows[...], jnp.zeros((CY - 16, ROWS), F32)], axis=0)
     halo_y[...] = stacked.T.reshape(NZ, CX, CY)
 
     def face(w, m, n, k, kn, up, drop):
@@ -294,12 +309,13 @@
             return lift + g, faces + c, beside + c * pn
 
         for side in range(2):
-            halo = hx_recv[side, z]
+            here = pl.ds(z, 1)
+            halo = [hx_mob[side, c, here, :] for c in range(3)] + [hx_recv[side, n, here, :] for n in (3, 4, 5, 0)]
             edge = 0 if side == 0 else CX - 1
             inside = (ix > 0) if side == 0 else (ix < NGX - 1)
 
             def shifted(f, n):
-                return jnp.where(row == edge, jnp.broadcast_to(halo[n:n + 1, :], (CX, CY)), pltpu.roll(f, 1 if side == 0 else CX - 1, 0))
+                return jnp.where(row == edge, jnp.broadcast_to(halo[n], (CX, CY)), pltpu.roll(f, 1 if side == 0 else CX - 1, 0))
             k = perm_ref[0, z]
             kn = shifted(k, 3)
             kn = jnp.where((row == edge) & jnp.logical_not(inside), 0.0, kn)
@@ -449,7 +465,8 @@
 
 
 def hand_over(p_src, bhp_src, p_dst, bhp_dst, sem):
-    copies = (pltpu.make_async_copy(p_src, p_dst, sem.at[0]), pltpu.make_async_copy(bhp_src, bhp_dst, sem.at[1]))
+    copies = [pltpu.make_async_copy(bhp_src, bhp_dst, sem.at[4])]
+    copies += [pltpu.make_async_copy(p_src.at[3 * n:3 * n + 3], p_dst.at[3 * n:3 * n + 3], sem.at[n]) for n in range(4)]
     for copy in copies:
         copy.start()
     for copy in copies:
@@ -483,6 +500,8 @@
             pltpu.VMEM((ROWS, SLOTS), BF16),
             pltpu.VMEM((ROWS, 4 * CY), BF16),
             pltpu.VMEM((CY, SLOTS), BF16),
+            pltpu.VMEM((CY, SLOTS), BF16),
+            pltpu.VMEM((32, SLOTS), BF16),
             pltpu.VMEM((128, SLOTS), BF16),
             pltpu.VMEM((SLOTS, SLOTS), BF16),
             pltpu.VMEM((6,) + grid, F32),
@@ -505,16 +524,18 @@
             pltpu.VMEM((NGX, 2, CY), F32),
             pltpu.VMEM((2, NGX, CY), F32),
             pltpu.VMEM((2, 2, 16, CY), F32),
-            pltpu.VMEM((2, NZ, 8, CY), F32),
-            pltpu.VMEM((2, NZ, 8, CY), F32),
+            pltpu.VMEM((2, 6, NZ, CY), F32),
+            pltpu.VMEM((2, 6, NZ, CY), F32),
+            pltpu.VMEM((2, 3, NZ, CY), F32),
             pltpu.VMEM((2, 8, ROWS), F32),
             pltpu.VMEM((2, 8, ROWS), F32),
+            pltpu.VMEM((16, ROWS), F32),
             pltpu.VMEM(grid, F32),
             pltpu.VMEM((2, NZ, 1, CY), F32),
             pltpu.VMEM((2, NZ, 1, CY), F32),
             pltpu.VMEM((2, 8, ROWS), F32),
             pltpu.VMEM((2, 8, ROWS), F32),
-            dma((12,)),
+            dma((13,)),
             dma((12,)),
             dma((12,)),
         ],
@@ -528,7 +549,7 @@
         out_shape=(jax.ShapeDtypeStruct(grid, F32), jax.ShapeDtypeStruct((1, 32), F32)),
         in_specs=[vmem] * 2,
         out_specs=(anywhere, anywhere),
-        scratch_shapes=[dma((2,))],
+        scratch_shapes=[dma((5,))],
         name="hand_over",
     )(pltpu.with_memory_space_constraint(new_pressure, pltpu.VMEM), pltpu.with_memory_space_constraint(well_bhp, pltpu.VMEM))
     return new_pressure, well_bhp.reshape(32)

time: 32.5 us -> 32.1 us (0.988)
  Pallas kernels: 31.7 us -> 31.3 us
    pallas_call x1, Pallas kernels: 31 us -> 30.6 us  [body(): pl.pallas_call(kernel, out_shape=(pltpu.VMEM(grid, F32), pltpu.VMEM((1, 3...]
where the time goes in v5:
time: 32.1 us; the launch traced here: 31.9 us
  Pallas kernels  31.3 us (98%)
  between operations  0.64 us (2%)
    pallas_call x1, Pallas kernels, body(): pl.pallas_call(kernel, out_shape=(pltpu.VMEM(grid, F32), pltpu.VMEM((1, 3...  30.6 us
    pallas_call x1, Pallas kernels, body(): pl.pallas_call(hand_over, out_shape=(jax.ShapeDtypeStruct(grid, F32), jax...  0.72 us

profile of v5, /device:TPU:1, one launch (start us, length us, event | category | flops | bytes accessed | tf_op | source)
XLA Modules:
  0.0 31.9 jit_solution(17779112307975930662)
XLA Ops:
  0.6 30.6 %cpr_step.1 = (f32[12,32,128]{2,1,0:T(8,128)S(1)}, f32[1,32]{1,0:T(1,128)S(1)}) custom-call(f32[12,32,128]{2,1,0:T(8,128)} %p_hbm.1, f32[2,12,32,128]{3,2,1,0:T(8,128)} %sat_hbm.1, f32[3,12,32,128]{3,2,1,0:T(8,128)} %perm_hbm.1, f32[12,32,128]{2,1,0:T(8,128)} %pv_hbm.1, f32[12,32,128]{2,1,0:T(8,128)} %dep_hbm.1, f32[3,12,32,128]{3,2,1,0:T(8,128)} %res_hbm.1, ...), custom_call_target="tpu_custom_call" | custom-call | tf_op jit(solution)/shard_map/cpr_step/pallas_call | solution.py:481
  31.2 0.7 %hand_over.1 = (f32[12,32,128]{2,1,0:T(8,128)}, f32[1,32]{1,0:T(1,128)}) custom-call(f32[12,32,128]{2,1,0:T(8,128)S(1)} %get-tuple-element.6.p_src, f32[1,32]{1,0:T(1,128)S(1)} %get-tuple-element.7.bhp_src), custom_call_target="tpu_custom_call" | custom-call | tf_op jit(solution)/shard_map/hand_over/pallas_call | solution.py:547

commit v6 on v5

--- a/solution.py
+++ b/solution.py
@@ -8,6 +8,7 @@
 MESH = pl.DeviceIdType.MESH
 NZ, CX, CY = 12, 32, 128
 ROWS = NZ * CX
+SENT_ROWS = 7 * (32 + 16) + 15 * (32 + 16) + 2 * 16 + (3 + 15) * 2 + 2 * (6 * NZ + 24) + 2 * (NZ + 24)
 SLOTS = 1024
 NGX, NGY = 16, 8
 GAMMA = (0.4, 0.5, 0.08)
@@ -47,7 +48,7 @@
     p_ref, sat_ref, perm_ref, pv_ref, dep_ref, res_ref, flag_ref, pc_ref, pw_ref, pi_ref, wm_ref, wt_ref,
     mob, onehot, fields, wlane, clane, wrow, wpart, same, coup, pre, inv, rhs, cur, wacc, slotv,
     table0, table1, rs_recv0, rs_recv1, xs_src0, xs_src1, xs_recv0, xs_recv1, pair_src, pair_recv, tm_all, ctl, ball,
-    hx_send, hx_recv, hx_mob, hy_send, hy_recv, hy_rows, halo_y, hx2_send, hx2_recv, hy2_send, hy2_recv,
+    hx_send, hx_recv, hx_mob, hy_send, hy_recv, hy_rows, halo_y, hx2_send, hx2_recv, hy2_send, hy2_recv, sent,
     in_sem, send_sem, recv_sem,
 ):
     ix, iy = lax.axis_index("gx"), lax.axis_index("gy")
@@ -60,15 +61,25 @@
     def gy_of(a, b):
         return lax.rem(chip_x + a, 4) * 2 + lax.rem(core + b, 2)
 
-    loads = {}
-    pairs = (("pc", pc_hbm, pc_ref), ("pw", pw_hbm, pw_ref), ("pi", pi_hbm, pi_ref), ("sw", sat_hbm.at[0], sat_ref.at[0]),
-             ("sg", sat_hbm.at[1], sat_ref.at[1]), ("p", p_hbm, p_ref), ("wm", wm_hbm, wm_ref), ("wt", wt_hbm, wt_ref),
-             ("perm", perm_hbm, perm_ref), ("dep", dep_hbm, dep_ref), ("flag", flag_hbm, flag_ref),
-             ("pv", pv_hbm, pv_ref), ("res", res_hbm, res_ref))
-    for n, (name, src, dst) in enumerate(pairs):
-        loads[name] = pltpu.make_async_copy(src, dst, in_sem.at[n])
-    for name in ("pc", "pw", "pi", "sw", "sg", "p"):
-        loads[name].start()
+    loads = (
+        ((pc_hbm, pc_ref), (pw_hbm, pw_ref), (pi_hbm, pi_ref)),
+        ((sat_hbm.at[0], sat_ref.at[0]), (sat_hbm.at[1], sat_ref.at[1]), (p_hbm, p_ref)),
+        ((wm_hbm, wm_ref),),
+        ((perm_hbm, perm_ref), (dep_hbm, dep_ref), (flag_hbm, flag_ref)),
+        ((pv_hbm, pv_ref), (res_hbm, res_ref)),
+        ((wt_hbm, wt_ref),),
+    )
+    sizes = (slotv.at[0:3], perm_ref, wm_ref, coup.at[0:5], coup.at[0:4], wt_ref)
+
+    def load(n):
+        for src, dst in loads[n]:
+            pltpu.make_async_copy(src, dst, in_sem.at[n]).start()
+
+    def loaded(n):
+        pltpu.make_async_copy(sizes[n], sizes[n], in_sem.at[n]).wait()
+
+    load(0)
+    load(1)
 
     barrier = pltpu.get_barrier_semaphore()
     for a, b in GX_OFFSETS:
@@ -76,8 +87,8 @@
     for a, b in GY_OFFSETS:
         pl.semaphore_signal(barrier, inc=1, device_id=(ix, gy_of(a, b)), device_id_type=MESH)
 
-    for name in ("wm", "wt", "perm", "dep", "flag", "pv", "res"):
-        loads[name].start()
+    for n in (2, 5, 3, 4):
+        load(n)
 
     lane = lax.broadcasted_iota(jnp.int32, (CX, CY), 1)
     row = lax.broadcasted_iota(jnp.int32, (CX, CY), 0)
@@ -94,18 +105,15 @@
 
     class Group:
         def __init__(self, sem, copies, whole):
-            self.copies = [remote(src, dst, send_sem.at[sem], recv_sem.at[sem], dev) for src, dst, dev in copies]
-            self.all = remote(whole, whole, send_sem.at[sem], recv_sem.at[sem], copies[0][2])
+            self.copies = [remote(src, dst, send_sem, recv_sem.at[sem], dev) for src, dst, dev in copies]
+            self.whole = (whole, whole, send_sem, recv_sem.at[sem], copies[0][2])
 
         def send(self):
             for copy in self.copies:
                 copy.start()
 
         def arrive(self):
-            self.all.wait_recv()
-
-        def left(self):
-            self.all.wait_send()
+            remote(*self.whole).wait_recv()
 
     rs = [Group(t, [(table[t].at[lax.rem(core + b, 2)], rs_recv[t].at[n], (ix, gy_of(a, b))) for n, (a, b) in enumerate(GY_OFFSETS)],
                 rs_recv[t]) for t in range(2)]
@@ -116,17 +124,16 @@
     pair = Group(6, [(pair_src, pair_recv.at[n], (ix, gy_of(a, b))) for n, (a, b) in enumerate(x_peers)], pair_recv)
     tm = Group(7, [(tm_all.at[ix], tm_all.at[ix], (gx_of(a, b), iy)) for a, b in GX_OFFSETS], tm_all.at[0:NGX - 1])
 
-    def halo_group(sem, xs, xr, ys, yr):
+    def halo_groups(sem, xs, xr, ys, yr, size):
         after, before = (lax.rem(ix + 1, NGX), iy), (lax.rem(ix + NGX - 1, NGX), iy)
         right, left = (ix, lax.rem(iy + 1, NGY)), (ix, lax.rem(iy + NGY - 1, NGY))
-        return (Group(sem, [(xs.at[1], xr.at[0], after), (xs.at[0], xr.at[1], before)], xr),
-                Group(sem + 1, [(ys.at[1], yr.at[0], right), (ys.at[0], yr.at[1], left)], yr))
-
-    halo1 = halo_group(8, hx_send, hx_recv, hy_send, hy_recv)
-    halo2 = halo_group(10, hx2_send, hx2_recv, hy2_send, hy2_recv)
-
-    for name in ("pc", "pw", "pi"):
-        loads[name].wait()
+        return (Group(sem, [(xs.at[1], xr.at[0], after), (xs.at[0], xr.at[1], before)], size),
+                Group(sem, [(ys.at[1], yr.at[0], right), (ys.at[0], yr.at[1], left)], size))
+
+    halo1 = halo_groups(8, hx_send, hx_recv, hy_send, hy_recv, coup.at[0, 0:6])
+    halo2 = halo_groups(9, hx2_send, hx2_recv, hy2_send, hy2_recv, hx_mob)
+
+    loaded(0)
     cell = pc_ref[...]
     cell_row = cell >> 7
     live = pw_ref[...] >= 0
@@ -147,8 +154,7 @@
 
     clane[...] = jnp.where(lax.broadcasted_iota(jnp.int32, (CY, SLOTS), 0) == (cell & 127), 1.0, 0.0).astype(BF16)
 
-    for name in ("sw", "sg", "p"):
-        loads[name].wait()
+    loaded(1)
 
     @pl.loop(0, NZ)
     def _(z):
@@ -195,8 +201,8 @@
     for n, sums in enumerate(well_sums((2, 1))):
         table0[:, 16 * n:16 * n + 16, :] = sums
 
-    loads["wm"].wait()
-    loads["wt"].wait()
+    loaded(2)
+    loaded(5)
     pair_lane = lax.broadcasted_iota(jnp.int32, (2, CY), 1)
     pair_row = lax.broadcasted_iota(jnp.int32, (2, CY), 0)
     target4 = jnp.broadcast_to(jnp.concatenate([wt_ref[...]] * 4, axis=1), (2, CY))
@@ -224,8 +230,7 @@
     pair.send()
     rs[0].send()
 
-    for name in ("perm", "dep", "flag"):
-        loads[name].wait()
+    loaded(3)
     for z in range(NZ):
         for side, edge in enumerate((0, CX - 1)):
             at = slice(edge, edge + 1)
@@ -266,10 +271,8 @@
     tm.send()
     exchange(0)
 
-    for name in ("pv", "res"):
-        loads[name].wait()
-    for group in halo1:
-        group.arrive()
+    loaded(4)
+    halo1[0].arrive()
     for side in range(2):
         for c, m in enumerate(phase_mobility(hx_recv[side, 0], hx_recv[side, 1], hx_recv[side, 2])):
             hx_mob[side, c] = m
@@ -429,8 +432,7 @@
         group.send()
     exchange(1)
 
-    for group in halo2:
-        group.arrive()
+    halo2[0].arrive()
     stacked = jnp.concatenate([hy2_recv[0], hy2_recv[1], jnp.zeros((CY - 16, ROWS), F32)], axis=0)
     halo_y[...] = stacked.T.reshape(NZ, CX, CY)
 
@@ -460,13 +462,11 @@
     mine = mine + pltpu.roll(mine, 32, 1) + pltpu.roll(mine, 64, 1) + pltpu.roll(mine, 96, 1)
     bhp_ref[...] = mine[0:1, 0:32]
 
-    for group in rs + xs + bh + [pair, tm] + list(halo1 + halo2):
-        group.left()
+    remote(sent, sent, send_sem, recv_sem.at[0], partner).wait_send()
 
 
 def hand_over(p_src, bhp_src, p_dst, bhp_dst, sem):
-    copies = [pltpu.make_async_copy(bhp_src, bhp_dst, sem.at[4])]
-    copies += [pltpu.make_async_copy(p_src.at[3 * n:3 * n + 3], p_dst.at[3 * n:3 * n + 3], sem.at[n]) for n in range(4)]
+    copies = (pltpu.make_async_copy(p_src, p_dst, sem.at[0]), pltpu.make_async_copy(bhp_src, bhp_dst, sem.at[1]))
     for copy in copies:
         copy.start()
     for copy in copies:
@@ -535,9 +535,10 @@
             pltpu.VMEM((2, NZ, 1, CY), F32),
             pltpu.VMEM((2, 8, ROWS), F32),
             pltpu.VMEM((2, 8, ROWS), F32),
-            dma((13,)),
-            dma((12,)),
-            dma((12,)),
+            pltpu.VMEM((SENT_ROWS, 1, CY), F32),
+            dma((6,)),
+            dma,
+            dma((10,)),
         ],
         compiler_params=pltpu.CompilerParams(collective_id=0, has_side_effects=True),
         name="cpr_step",
@@ -549,7 +550,7 @@
         out_shape=(jax.ShapeDtypeStruct(grid, F32), jax.ShapeDtypeStruct((1, 32), F32)),
         in_specs=[vmem] * 2,
         out_specs=(anywhere, anywhere),
-        scratch_shapes=[dma((5,))],
+        scratch_shapes=[dma((2,))],
         name="hand_over",
     )(pltpu.with_memory_space_constraint(new_pressure, pltpu.VMEM), pltpu.with_memory_space_constraint(well_bhp, pltpu.VMEM))
     return new_pressure, well_bhp.reshape(32)

time: 32.1 us -> 31.9 us (level)
  no operation moved by 1% of the time
where the time goes in v6:
time: 31.9 us; the launch traced here: 31.7 us
  Pallas kernels  31.1 us (97%)
  between operations  0.64 us (2%)
    pallas_call x1, Pallas kernels, body(): pl.pallas_call(kernel, out_shape=(pltpu.VMEM(grid, F32), pltpu.VMEM((1, 3...  30.4 us
    pallas_call x1, Pallas kernels, body(): pl.pallas_call(hand_over, out_shape=(jax.ShapeDtypeStruct(grid, F32), jax...  0.7 us

profile of v6, /device:TPU:1, one launch (start us, length us, event | category | flops | bytes accessed | tf_op | source)
XLA Modules:
  0.0 31.7 jit_solution(10686054794783315360)
XLA Ops:
  0.6 30.4 %cpr_step.1 = (f32[12,32,128]{2,1,0:T(8,128)S(1)}, f32[1,32]{1,0:T(1,128)S(1)}) custom-call(f32[12,32,128]{2,1,0:T(8,128)} %p_hbm.1, f32[2,12,32,128]{3,2,1,0:T(8,128)} %sat_hbm.1, f32[3,12,32,128]{3,2,1,0:T(8,128)} %perm_hbm.1, f32[12,32,128]{2,1,0:T(8,128)} %pv_hbm.1, f32[12,32,128]{2,1,0:T(8,128)} %dep_hbm.1, f32[3,12,32,128]{3,2,1,0:T(8,128)} %res_hbm.1, ...), custom_call_target="tpu_custom_call" | custom-call | tf_op jit(solution)/shard_map/cpr_step/pallas_call | solution.py:481
  31.0 0.7 %hand_over.1 = (f32[12,32,128]{2,1,0:T(8,128)}, f32[1,32]{1,0:T(1,128)}) custom-call(f32[12,32,128]{2,1,0:T(8,128)S(1)} %get-tuple-element.6.p_src, f32[1,32]{1,0:T(1,128)S(1)} %get-tuple-element.7.bhp_src), custom_call_target="tpu_custom_call" | custom-call | tf_op jit(solution)/shard_map/hand_over/pallas_call | solution.py:548

commit v7 on v6

--- a/solution.py
+++ b/solution.py
@@ -397,9 +397,12 @@
         bh[t].arrive()
         wells = ball[t].reshape(32, CY)
         high, low = split(wells)
-        g = jnp.dot(jnp.concatenate([high, low], axis=0), wlane[...], preferred_element_type=F32)
-        slot_bhp = jnp.sum(jnp.where(well_rows, g[0:32] + g[32:64], 0.0), axis=0, keepdims=True)
-        slotv[2:3, :] = slotv[1:2, :] * slot_bhp
+        both = jnp.concatenate([high, low], axis=0)
+        for j in range(SLOTS // 256):
+            chunk = slice(j * 256, (j + 1) * 256)
+            g = jnp.dot(both, wlane[:, chunk], preferred_element_type=F32)
+            slot_bhp = jnp.sum(jnp.where(well_rows[:, chunk], g[0:32] + g[32:64], 0.0), axis=0, keepdims=True)
+            slotv[2:3, chunk] = slotv[1:2, chunk] * slot_bhp
 
     sums = finish_sums(0)
     base = sums[16:32]
@@ -407,9 +410,10 @@
     bh[0].send()
     slot_flow(0)
     high, low = split(slotv[2:3, :])
-    flow = jnp.concatenate([jnp.broadcast_to(high, (16, SLOTS)), jnp.broadcast_to(low, (16, SLOTS))], axis=0)
+    upper = lax.broadcasted_iota(jnp.int32, (16, SLOTS), 0) < 8
+    flow = jnp.where(upper, high.astype(F32), low.astype(F32)).astype(BF16)
     met = jnp.dot(flow, same[...], preferred_element_type=F32)
-    slotv[6:7, :] = slotv[1:2, :] * (slotv[4:5, :] + slotv[5:6, :] * (met[0:1, :] + met[16:17, :]))
+    slotv[6:7, :] = slotv[1:2, :] * (slotv[4:5, :] + slotv[5:6, :] * (met[0:1, :] + met[8:9, :]))
     table1[...] = well_sums((6,))[0]
     rs[1].send()
 

time: 31.9 us -> 31.8 us (level)
  no operation moved by 1% of the time
where the time goes in v7:
time: 31.8 us; the launch traced here: 31.6 us
  Pallas kernels  31 us (97%)
  between operations  0.64 us (2%)
    pallas_call x1, Pallas kernels, body(): pl.pallas_call(kernel, out_shape=(pltpu.VMEM(grid, F32), pltpu.VMEM((1, 3...  30.3 us
    pallas_call x1, Pallas kernels, body(): pl.pallas_call(hand_over, out_shape=(jax.ShapeDtypeStruct(grid, F32), jax...  0.7 us

profile of v7, /device:TPU:1, one launch (start us, length us, event | category | flops | bytes accessed | tf_op | source)
XLA Modules:
  0.0 31.6 jit_solution(3918275705668490151)
XLA Ops:
  0.6 30.3 %cpr_step.1 = (f32[12,32,128]{2,1,0:T(8,128)S(1)}, f32[1,32]{1,0:T(1,128)S(1)}) custom-call(f32[12,32,128]{2,1,0:T(8,128)} %p_hbm.1, f32[2,12,32,128]{3,2,1,0:T(8,128)} %sat_hbm.1, f32[3,12,32,128]{3,2,1,0:T(8,128)} %perm_hbm.1, f32[12,32,128]{2,1,0:T(8,128)} %pv_hbm.1, f32[12,32,128]{2,1,0:T(8,128)} %dep_hbm.1, f32[3,12,32,128]{3,2,1,0:T(8,128)} %res_hbm.1, ...), custom_call_target="tpu_custom_call" | custom-call | tf_op jit(solution)/shard_map/cpr_step/pallas_call | solution.py:485
  30.9 0.7 %hand_over.1 = (f32[12,32,128]{2,1,0:T(8,128)}, f32[1,32]{1,0:T(1,128)}) custom-call(f32[12,32,128]{2,1,0:T(8,128)S(1)} %get-tuple-element.6.p_src, f32[1,32]{1,0:T(1,128)S(1)} %get-tuple-element.7.bhp_src), custom_call_target="tpu_custom_call" | custom-call | tf_op jit(solution)/shard_map/hand_over/pallas_call | solution.py:552
